TPU v7x, 32 devices: a whole 2x2x4 slice. The times are simulated.
32 devices in a mesh: dp: 8 (over z, y), tensor: 4 (over x, core).
Axes of the slice: x: 2, y: 2, z: 4, core: 2. Of those that a mesh axis runs over, the one named last changes fastest.
Arguments:
- frames_in: bfloat16 [4096, 1024], P(('dp', 'tensor')), may hold values from -6 to 6
- codes_in: bfloat16 [4096, 3, 1024], P(('dp', 'tensor')), may hold values from -6 to 6
- lengths: int32 [8], P('dp'), may hold values from 64 to 512, as said below
- outer_gain: bfloat16 [1024], replicated, may hold values from 0.099609375 to 1.8984375
- outer_query: bfloat16 [1024, 1024], P(None, 'tensor'), may hold values from -0.1875 to 0.1875
- outer_key: bfloat16 [1024, 1024], P(None, 'tensor'), may hold values from -0.1875 to 0.1875
- outer_value: bfloat16 [1024, 1024], P(None, 'tensor'), may hold values from -0.1875 to 0.1875
- outer_merge: bfloat16 [1024, 1024], P('tensor'), may hold values from -1 to 1
- outer_scale: bfloat16 [1024], replicated, may hold values from 0.099609375 to 1.8984375
- outer_up: bfloat16 [1024, 4096], P(None, 'tensor'), may hold values from -0.1875 to 0.1875
- outer_shift: bfloat16 [4096], P('tensor'), may hold values from -3 to 3
- outer_down: bfloat16 [4096, 1024], P('tensor'), may hold values from -0.09375 to 0.09375
- outer_offset: bfloat16 [1024], replicated, may hold values from -2 to 2
- inner_gain: bfloat16 [1024], replicated, may hold values from 0.099609375 to 1.8984375
- inner_query: bfloat16 [1024, 1024], P(None, 'tensor'), may hold values from -0.1875 to 0.1875
- inner_key: bfloat16 [1024, 1024], P(None, 'tensor'), may hold values from -0.1875 to 0.1875
- inner_value: bfloat16 [1024, 1024], P(None, 'tensor'), may hold values from -0.1875 to 0.1875
- inner_merge: bfloat16 [1024, 1024], P('tensor'), may hold values from -0.25 to 0.25
- inner_scale: bfloat16 [1024], replicated, may hold values from 0.099609375 to 1.8984375
- inner_up: bfloat16 [1024, 4096], P(None, 'tensor'), may hold values from -0.1875 to 0.1875
- inner_shift: bfloat16 [4096], P('tensor'), may hold values from -3 to 3
- inner_down: bfloat16 [4096, 1024], P('tensor'), may hold values from -0.09375 to 0.09375
- inner_offset: bfloat16 [1024], replicated, may hold values from -2 to 2
- cot_global: bfloat16 [4096, 1024], P(('dp', 'tensor')), may hold values from -6 to 6
- cot_local: bfloat16 [4096, 4, 1024], P(('dp', 'tensor')), may hold values from -6 to 6
Outputs:
- global_out: float32 [4096, 1024], P(('dp', 'tensor'))
- local_out: float32 [4096, 4, 1024], P(('dp', 'tensor'))
- grad_frames: float32 [4096, 1024], P(('dp', 'tensor'))
- grad_codes: float32 [4096, 3, 1024], P(('dp', 'tensor'))
- outergain_grad: float32 [1024], replicated
- outerquery_grad: float32 [1024, 1024], P('dp', 'tensor')
- outerkey_grad: float32 [1024, 1024], P('dp', 'tensor')
- outervalue_grad: float32 [1024, 1024], P('dp', 'tensor')
- outermerge_grad: float32 [1024, 1024], P('tensor', 'dp')
- outerscale_grad: float32 [1024], replicated
- outerup_grad: float32 [1024, 4096], P('dp', 'tensor')
- outershift_grad: float32 [4096], replicated
- outerdown_grad: float32 [4096, 1024], P('tensor', 'dp')
- outeroffset_grad: float32 [1024], replicated
- innergain_grad: float32 [1024], replicated
- innerquery_grad: float32 [1024, 1024], P('dp', 'tensor')
- innerkey_grad: float32 [1024, 1024], P('dp', 'tensor')
- innervalue_grad: float32 [1024, 1024], P('dp', 'tensor')
- innermerge_grad: float32 [1024, 1024], P('tensor', 'dp')
- innerscale_grad: float32 [1024], replicated
- innerup_grad: float32 [1024, 4096], P('dp', 'tensor')
- innershift_grad: float32 [4096], replicated
- innerdown_grad: float32 [4096, 1024], P('tensor', 'dp')
- inneroffset_grad: float32 [1024], replicated
Inputs may be any that keep to these rules, and one draw needn't show every extreme that they name: Utterance u has its first lengths[u] frames valid and the rest padding; some utterance has exactly 512 valid frames and some exactly 64.
All inputs are finite; a program needn't handle non-finite values.
Results may differ from a plain program's by a relative error of at most 0.02.
Values may be sent and summed in bfloat16 or wider, within the bound.
No kernel may reach another device: no remote copies, remote signals or barrier semaphores. Data moves between devices by JAX's collectives and lax.ppermute only.
A program may use at most 256 MiB of HBM per device.

v0:
```python
import jax
import jax.numpy as jnp
from jax import lax
from jax.sharding import PartitionSpec as P

HEAD_DIM = 64
FF = 4096
SLOTS = 4


EPSILON = 1e-05
MASKED = -1e30


def norm_rows(values, norm_gain):
    return (
        values * lax.rsqrt(jnp.mean(values * values, axis=-1, keepdims=True) + EPSILON) * norm_gain
    )


def outer_attend(query_proj, key_proj, value_proj):
    length = query_proj.shape[0]
    heads_here = query_proj.shape[1] // HEAD_DIM
    block_len = min(512, length)
    score_scale = HEAD_DIM ** (-0.5)
    query_heads = query_proj.reshape(length, heads_here, HEAD_DIM)
    key_heads = key_proj.reshape(length, heads_here, HEAD_DIM)
    value_heads = value_proj.reshape(length, heads_here, HEAD_DIM)
    col_pos = jnp.arange(length, dtype=jnp.int32)

    def one_block(row_start):
        scores = (
            jnp.einsum("qhd,khd->hqk", query_heads, key_heads, preferred_element_type=jnp.float32)
            * score_scale
        )
        row_pos = row_start + jnp.arange(block_len, dtype=jnp.int32)
        scores = jnp.where(col_pos[None, None, :] <= row_pos[None, :, None], scores, MASKED)
        largest = jnp.max(scores, axis=-1, keepdims=True)
        raised = jnp.exp(scores - largest)
        row_total = jnp.sum(raised, axis=-1, keepdims=True)
        attn_probs = (raised / row_total).astype(jnp.bfloat16)
        context = jnp.einsum(
            "hqk,khd->qhd", attn_probs, value_heads, preferred_element_type=jnp.float32
        )
        return (context.astype(jnp.bfloat16), (largest + jnp.log(row_total))[:, :, 0])

    block_starts = jnp.arange(length // block_len, dtype=jnp.int32) * block_len
    contexts, logsum = lax.map(one_block, block_starts)
    return (contexts.reshape(length, heads_here * HEAD_DIM), logsum)


def outer_attend_back(query_proj, key_proj, value_proj, logsum, grad_context):
    length = query_proj.shape[0]
    heads_here = query_proj.shape[1] // HEAD_DIM
    block_len = min(512, length)
    score_scale = HEAD_DIM ** (-0.5)
    query_heads = query_proj.reshape(length, heads_here, HEAD_DIM)
    key_heads = key_proj.reshape(length, heads_here, HEAD_DIM)
    value_heads = value_proj.reshape(length, heads_here, HEAD_DIM)
    grad_heads = grad_context.reshape(length, heads_here, HEAD_DIM)
    col_pos = jnp.arange(length, dtype=jnp.int32)

    def one_block(running, block_in):
        grad_key, grad_value = running
        row_start, block_lse = block_in
        scores = (
            jnp.einsum("qhd,khd->hqk", query_heads, key_heads, preferred_element_type=jnp.float32)
            * score_scale
        )
        row_pos = row_start + jnp.arange(block_len, dtype=jnp.int32)
        scores = jnp.where(col_pos[None, None, :] <= row_pos[None, :, None], scores, MASKED)
        attn_probs = jnp.exp(scores - block_lse[:, :, None])
        grad_probs = jnp.einsum(
            "qhd,khd->hqk", grad_heads, value_heads, preferred_element_type=jnp.float32
        )
        row_inner = jnp.sum(attn_probs * grad_probs, axis=-1, keepdims=True)
        grad_scores = (attn_probs * (grad_probs - row_inner)).astype(jnp.bfloat16)
        grad_query = (
            jnp.einsum("hqk,khd->qhd", grad_scores, key_heads, preferred_element_type=jnp.float32)
            * score_scale
        )
        grad_key = (
            grad_key
            + jnp.einsum(
                "hqk,qhd->khd", grad_scores, query_heads, preferred_element_type=jnp.float32
            )
            * score_scale
        )
        grad_value = grad_value + jnp.einsum(
            "hqk,qhd->khd",
            attn_probs.astype(jnp.bfloat16),
            grad_heads,
            preferred_element_type=jnp.float32,
        )
        return ((grad_key, grad_value), grad_query)

    block_starts = jnp.arange(length // block_len, dtype=jnp.int32) * block_len
    empty_grad = jnp.zeros((length, heads_here, HEAD_DIM), jnp.float32)
    (grad_key, grad_value), grad_query = lax.scan(
        one_block, (empty_grad, empty_grad), (block_starts, logsum)
    )
    flat_shape = (length, heads_here * HEAD_DIM)
    return (
        grad_query.reshape(flat_shape).astype(jnp.bfloat16),
        grad_key.reshape(flat_shape).astype(jnp.bfloat16),
        grad_value.reshape(flat_shape).astype(jnp.bfloat16),
    )


def inner_probs(query_slots, key_slots):
    score_scale = HEAD_DIM ** (-0.5)
    scores = (
        jnp.einsum("fqhd,fkhd->hqkf", query_slots, key_slots, preferred_element_type=jnp.float32)
        * score_scale
    )
    slot_ids = jnp.arange(SLOTS, dtype=jnp.int32)
    allowed = slot_ids[None, :] <= slot_ids[:, None]
    scores = jnp.where(allowed[None, :, :, None], scores, MASKED)
    largest = jnp.max(scores, axis=2, keepdims=True)
    raised = jnp.exp(scores - largest)
    return raised / jnp.sum(raised, axis=2, keepdims=True)


def inner_attend(query_proj, key_proj, value_proj):
    frames = query_proj.shape[0] // SLOTS
    heads_here = query_proj.shape[1] // HEAD_DIM
    shaped = (frames, SLOTS, heads_here, HEAD_DIM)
    attn_probs = inner_probs(query_proj.reshape(shaped), key_proj.reshape(shaped))
    context = jnp.einsum(
        "hqkf,fkhd->fqhd",
        attn_probs.astype(jnp.bfloat16),
        value_proj.reshape(shaped),
        preferred_element_type=jnp.float32,
    )
    return (context.reshape(query_proj.shape).astype(jnp.bfloat16), jnp.zeros((), jnp.float32))


def inner_attend_back(query_proj, key_proj, value_proj, unused, grad_context):
    frames = query_proj.shape[0] // SLOTS
    heads_here = query_proj.shape[1] // HEAD_DIM
    shaped = (frames, SLOTS, heads_here, HEAD_DIM)
    score_scale = HEAD_DIM ** (-0.5)
    query_slots = query_proj.reshape(shaped)
    key_slots = key_proj.reshape(shaped)
    grad_slots = grad_context.reshape(shaped)
    attn_probs = inner_probs(query_slots, key_slots)
    grad_probs = jnp.einsum(
        "fqhd,fkhd->hqkf",
        grad_slots,
        value_proj.reshape(shaped),
        preferred_element_type=jnp.float32,
    )
    row_inner = jnp.sum(attn_probs * grad_probs, axis=2, keepdims=True)
    grad_scores = (attn_probs * (grad_probs - row_inner)).astype(jnp.bfloat16)
    grad_query = (
        jnp.einsum("hqkf,fkhd->fqhd", grad_scores, key_slots, preferred_element_type=jnp.float32)
        * score_scale
    )
    grad_key = (
        jnp.einsum("hqkf,fqhd->fkhd", grad_scores, query_slots, preferred_element_type=jnp.float32)
        * score_scale
    )
    grad_value = jnp.einsum(
        "hqkf,fqhd->fkhd",
        attn_probs.astype(jnp.bfloat16),
        grad_slots,
        preferred_element_type=jnp.float32,
    )
    flat_shape = query_proj.shape
    return (
        grad_query.reshape(flat_shape).astype(jnp.bfloat16),
        grad_key.reshape(flat_shape).astype(jnp.bfloat16),
        grad_value.reshape(flat_shape).astype(jnp.bfloat16),
    )


def outer_spread(values):
    return lax.all_gather(values, "tensor", axis=0, tiled=True)


def outer_collect(make_rows, row_count):
    return lax.psum_scatter(
        make_rows(jnp.int32(0), row_count * lax.axis_size("tensor")),
        "tensor",
        scatter_dimension=0,
        tiled=True,
    )


def outer_spread_grad(values):
    return lax.all_gather(values, "tensor", axis=0, tiled=True)


def outer_collect_grad(make_rows, row_count):
    return lax.psum_scatter(
        make_rows(jnp.int32(0), row_count * lax.axis_size("tensor")).astype(jnp.bfloat16),
        "tensor",
        scatter_dimension=0,
        tiled=True,
    ).astype(jnp.float32)


def inner_spread(values):
    return lax.all_gather(values, "tensor", axis=0, tiled=True)


def inner_collect(make_rows, row_count):
    return lax.psum_scatter(
        make_rows(jnp.int32(0), row_count * lax.axis_size("tensor")),
        "tensor",
        scatter_dimension=0,
        tiled=True,
    )


def inner_spread_grad(values):
    return lax.all_gather(values, "tensor", axis=0, tiled=True)


def inner_collect_grad(make_rows, row_count):
    return lax.psum_scatter(
        make_rows(jnp.int32(0), row_count * lax.axis_size("tensor")),
        "tensor",
        scatter_dimension=0,
        tiled=True,
    )


def block_forward(rows_in, weights, attend, spread, collect):
    gain_attn, w_query, w_key, w_value, w_merge, gain_mlp, w_up, up_bias, w_down, down_bias = (
        weights
    )
    row_count = rows_in.shape[0]
    head_cols = w_query.shape[1]
    gathered = spread(norm_rows(rows_in, gain_attn.astype(jnp.float32)).astype(jnp.bfloat16))
    joined_w = jnp.concatenate([w_query, w_key, w_value], axis=1)
    projected = jnp.dot(gathered, joined_w, preferred_element_type=jnp.float32).astype(jnp.bfloat16)
    query_proj = projected[:, :head_cols]
    key_proj = projected[:, head_cols : 2 * head_cols]
    value_proj = projected[:, 2 * head_cols :]
    context, logsum = attend(query_proj, key_proj, value_proj)

    def merge_rows(row_start, count_rows):
        return jnp.dot(context, w_merge, preferred_element_type=jnp.float32)

    middle = rows_in + collect(merge_rows, row_count)
    gathered_mlp = spread(norm_rows(middle, gain_mlp.astype(jnp.float32)).astype(jnp.bfloat16))
    hidden_pre = jnp.dot(gathered_mlp, w_up, preferred_element_type=jnp.float32) + up_bias.astype(
        jnp.float32
    )
    hidden_low = jax.nn.gelu(hidden_pre).astype(jnp.bfloat16)

    def down_rows(row_start, count_rows):
        return jnp.dot(hidden_low, w_down, preferred_element_type=jnp.float32)

    output = middle + collect(down_rows, row_count) + down_bias.astype(jnp.float32)
    stored = (
        rows_in,
        middle,
        gathered,
        joined_w,
        query_proj,
        key_proj,
        value_proj,
        context,
        logsum,
        gathered_mlp,
        hidden_pre,
        hidden_low,
    )
    return (output, stored)


def block_backward(grad_output, weights, stored, attend_back, spread_grad, collect_grad):
    gain_attn, w_query, w_key, w_value, w_merge, gain_mlp, w_up, up_bias, w_down, down_bias = (
        weights
    )
    (
        rows_in,
        middle,
        gathered,
        joined_w,
        query_proj,
        key_proj,
        value_proj,
        context,
        logsum,
        gathered_mlp,
        hidden_pre,
        hidden_low,
    ) = stored
    row_count = grad_output.shape[0]
    head_cols = w_query.shape[1]
    grad_offset = jnp.sum(grad_output, axis=0)
    grad_full = spread_grad(grad_output.astype(jnp.bfloat16))
    grad_down = jnp.einsum("nk,nd->kd", hidden_low, grad_full, preferred_element_type=jnp.float32)
    grad_hidden = jnp.einsum("nd,kd->nk", grad_full, w_down, preferred_element_type=jnp.float32)
    grad_pre = jax.vjp(jax.nn.gelu, hidden_pre)[1](grad_hidden)[0].astype(jnp.bfloat16)
    grad_shift = jnp.sum(grad_pre, axis=0, dtype=jnp.float32)
    grad_up = jnp.einsum("nd,nk->dk", gathered_mlp, grad_pre, preferred_element_type=jnp.float32)

    def up_rows(row_start, count_rows):
        return jnp.einsum("nk,dk->nd", grad_pre, w_up, preferred_element_type=jnp.float32)

    grad_normed_mlp = collect_grad(up_rows, row_count)
    norm_pull = jax.vjp(norm_rows, middle, gain_mlp.astype(jnp.float32))[1]
    grad_middle_norm, grad_gain_mlp = norm_pull(grad_normed_mlp)
    grad_middle = grad_output + grad_middle_norm
    grad_branch = spread_grad(grad_middle.astype(jnp.bfloat16))
    grad_merge = jnp.einsum("nc,nd->cd", context, grad_branch, preferred_element_type=jnp.float32)
    grad_context = jnp.einsum(
        "nd,cd->nc", grad_branch, w_merge, preferred_element_type=jnp.float32
    ).astype(jnp.bfloat16)
    grad_query, grad_key, grad_value = attend_back(
        query_proj, key_proj, value_proj, logsum, grad_context
    )
    grad_joined = jnp.concatenate([grad_query, grad_key, grad_value], axis=1)
    grad_joined_w = jnp.einsum(
        "nd,nc->dc", gathered, grad_joined, preferred_element_type=jnp.float32
    )

    def project_rows(row_start, count_rows):
        return jnp.einsum("nc,dc->nd", grad_joined, joined_w, preferred_element_type=jnp.float32)

    grad_normed = collect_grad(project_rows, row_count)
    attn_pull = jax.vjp(norm_rows, rows_in, gain_attn.astype(jnp.float32))[1]
    grad_rows_norm, grad_gain_attn = attn_pull(grad_normed)
    grad_rows = grad_middle + grad_rows_norm
    grads = (
        grad_gain_attn,
        grad_joined_w[:, :head_cols],
        grad_joined_w[:, head_cols : 2 * head_cols],
        grad_joined_w[:, 2 * head_cols :],
        grad_merge,
        grad_gain_mlp,
        grad_up,
        grad_shift,
        grad_down,
        grad_offset,
    )
    return (grad_rows, grads)


def place_columns(values):
    column_count = values.shape[0]
    return lax.dynamic_update_slice(
        jnp.zeros((FF,), jnp.float32), values, (lax.axis_index("tensor") * column_count,)
    )


def per_device(
    frames_in,
    codes_in,
    lengths,
    outer_gain,
    outer_query,
    outer_key,
    outer_value,
    outer_merge,
    outer_scale,
    outer_up,
    outer_shift,
    outer_down,
    outer_offset,
    inner_gain,
    inner_query,
    inner_key,
    inner_value,
    inner_merge,
    inner_scale,
    inner_up,
    inner_shift,
    inner_down,
    inner_offset,
    cot_global,
    cot_local,
):
    outer_weights = (
        outer_gain,
        outer_query,
        outer_key,
        outer_value,
        outer_merge,
        outer_scale,
        outer_up,
        outer_shift,
        outer_down,
        outer_offset,
    )
    row_count = frames_in.shape[0]
    positions = lax.axis_index("tensor") * row_count + jnp.arange(row_count, dtype=jnp.int32)
    valid_rows = (positions < lengths[0]).astype(jnp.float32)
    global_rows, outer_stored = block_forward(
        frames_in.astype(jnp.float32), outer_weights, outer_attend, outer_spread, outer_collect
    )
    sequence = jnp.concatenate(
        [global_rows[:, None, :], codes_in.astype(jnp.float32)], axis=1
    ).reshape(row_count * SLOTS, -1)
    grad_local = (cot_local.astype(jnp.float32) * valid_rows[:, None, None]).reshape(
        row_count * SLOTS, -1
    )
    inner_weights = (
        inner_gain,
        inner_query,
        inner_key,
        inner_value,
        inner_merge,
        inner_scale,
        inner_up,
        inner_shift,
        inner_down,
        inner_offset,
    )
    local_rows, inner_stored = block_forward(
        sequence, inner_weights, inner_attend, inner_spread, inner_collect
    )
    grad_sequence, inner_grads = block_backward(
        grad_local,
        inner_weights,
        inner_stored,
        inner_attend_back,
        inner_spread_grad,
        inner_collect_grad,
    )
    inner_shift_full = place_columns(inner_grads[7])
    grad_sequence = grad_sequence.reshape(row_count, SLOTS, -1)
    grad_global = cot_global.astype(jnp.float32) * valid_rows[:, None] + grad_sequence[:, 0, :]
    grad_frames, outer_grads = block_backward(
        grad_global,
        outer_weights,
        outer_stored,
        outer_attend_back,
        outer_spread_grad,
        outer_collect_grad,
    )
    reduced = (
        lax.psum_scatter(
            outer_grads[1].astype(jnp.bfloat16), "dp", scatter_dimension=0, tiled=True
        ).astype(jnp.float32),
        lax.psum_scatter(
            outer_grads[2].astype(jnp.bfloat16), "dp", scatter_dimension=0, tiled=True
        ).astype(jnp.float32),
        lax.psum_scatter(
            outer_grads[3].astype(jnp.bfloat16), "dp", scatter_dimension=0, tiled=True
        ).astype(jnp.float32),
        lax.psum_scatter(
            outer_grads[4].astype(jnp.bfloat16), "dp", scatter_dimension=1, tiled=True
        ).astype(jnp.float32),
        lax.psum_scatter(
            outer_grads[6].astype(jnp.bfloat16), "dp", scatter_dimension=0, tiled=True
        ).astype(jnp.float32),
        lax.psum_scatter(
            outer_grads[8].astype(jnp.bfloat16), "dp", scatter_dimension=1, tiled=True
        ).astype(jnp.float32),
        lax.psum_scatter(
            inner_grads[1].astype(jnp.bfloat16), "dp", scatter_dimension=0, tiled=True
        ).astype(jnp.float32),
        lax.psum_scatter(
            inner_grads[2].astype(jnp.bfloat16), "dp", scatter_dimension=0, tiled=True
        ).astype(jnp.float32),
        lax.psum_scatter(
            inner_grads[3].astype(jnp.bfloat16), "dp", scatter_dimension=0, tiled=True
        ).astype(jnp.float32),
        lax.psum_scatter(
            inner_grads[4].astype(jnp.bfloat16), "dp", scatter_dimension=1, tiled=True
        ).astype(jnp.float32),
        lax.psum_scatter(
            inner_grads[6].astype(jnp.bfloat16), "dp", scatter_dimension=0, tiled=True
        ).astype(jnp.float32),
        lax.psum_scatter(
            inner_grads[8].astype(jnp.bfloat16), "dp", scatter_dimension=1, tiled=True
        ).astype(jnp.float32),
    )
    inner_mats = reduced[6:]
    vectors = lax.psum(
        (
            outer_grads[0],
            outer_grads[5],
            place_columns(outer_grads[7]),
            outer_grads[9],
            inner_grads[0],
            inner_grads[5],
            inner_shift_full,
            inner_grads[9],
        ),
        ("dp", "tensor"),
    )
    return (
        global_rows * valid_rows[:, None],
        local_rows.reshape(row_count, SLOTS, -1) * valid_rows[:, None, None],
        grad_frames,
        grad_sequence[:, 1:, :],
        vectors[0],
        reduced[0],
        reduced[1],
        reduced[2],
        reduced[3],
        vectors[1],
        reduced[4],
        vectors[2],
        reduced[5],
        vectors[3],
        vectors[4],
        inner_mats[0],
        inner_mats[1],
        inner_mats[2],
        inner_mats[3],
        vectors[5],
        inner_mats[4],
        vectors[6],
        inner_mats[5],
        vectors[7],
    )


def solution(mesh):
    in_specs = (
        P(("dp", "tensor"), None),
        P(("dp", "tensor"), None, None),
        P("dp"),
        P(),
        P(None, "tensor"),
        P(None, "tensor"),
        P(None, "tensor"),
        P("tensor", None),
        P(),
        P(None, "tensor"),
        P("tensor"),
        P("tensor", None),
        P(),
        P(),
        P(None, "tensor"),
        P(None, "tensor"),
        P(None, "tensor"),
        P("tensor", None),
        P(),
        P(None, "tensor"),
        P("tensor"),
        P("tensor", None),
        P(),
        P(("dp", "tensor"), None),
        P(("dp", "tensor"), None, None),
    )
    out_specs = (
        P(("dp", "tensor"), None),
        P(("dp", "tensor"), None, None),
        P(("dp", "tensor"), None),
        P(("dp", "tensor"), None, None),
        P(),
        P("dp", "tensor"),
        P("dp", "tensor"),
        P("dp", "tensor"),
        P("tensor", "dp"),
        P(),
        P("dp", "tensor"),
        P(),
        P("tensor", "dp"),
        P(),
        P(),
        P("dp", "tensor"),
        P("dp", "tensor"),
        P("dp", "tensor"),
        P("tensor", "dp"),
        P(),
        P("dp", "tensor"),
        P(),
        P("tensor", "dp"),
        P(),
    )
    return jax.shard_map(
        per_device, mesh=mesh, in_specs=in_specs, out_specs=out_specs, check_vma=False
    )
```

profile of v0, /device:TPU:0, one launch (start us, length us, event | category | flops | bytes accessed | tf_op | source)
XLA Modules:
  0.0 1671.0 jit_solution(2345448129182834943)
XLA Ops:
  16.0 15.8 all-gather.9.cloned.1.call-done
  41.5 31.5 %reduce-scatter.29.cloned.1.call-done = f32[128,1024]{1,0:T(8,128)} async-done(((f32[512,1024]{1,0:T(8,128)}), f32[128,1024]{1,0:T(8,128)}) %reduce-scatter.29.cloned.1.call-update) | async-done | bytes 524304 | tf_op jit(solution)/shard_map/reduce_scatter | solution.py:182
  75.7 16.8 %all-gather.11.cloned.1.call-done = bf16[512,1024]{1,0:T(8,128)(2,1)} async-done(((bf16[128,1024]{1,0:T(8,128)(2,1)}), bf16[512,1024]{1,0:T(8,128)(2,1)}) %all-gather.11.cloned.1.call-update) | async-done | bytes 1048592 | tf_op jit(solution)/shard_map/all_gather | solution.py:178
  102.5 29.1 %reduce-scatter.31.cloned.1.call-done = f32[128,1024]{1,0:T(8,128)} async-done(((f32[512,1024]{1,0:T(8,128)}), f32[128,1024]{1,0:T(8,128)}) %reduce-scatter.31.cloned.1.call-update) | async-done | bytes 524304 | tf_op jit(solution)/shard_map/reduce_scatter | solution.py:182
  135.5 4.2 copy.129
  148.5 31.7 %all-gather.13.cloned.1.call-done = bf16[2048,1024]{1,0:T(8,128)(2,1)} async-done(((bf16[512,1024]{1,0:T(8,128)(2,1)}), bf16[2048,1024]{1,0:T(8,128)(2,1)}) %all-gather.13.cloned.1.call-update) | async-done | bytes 4194320 | tf_op jit(solution)/shard_map/all_gather | solution.py:204
  180.2 6.1 convolution_convert_fusion
  187.9 4.5 reshape.271
  192.3 4.4 reshape.273
  198.6 6.5 fusion.31
  211.9 4.4 convert_bitcast_fusion.1
  222.2 5.6 fusion.103
  228.5 71.2 %reduce-scatter.33.cloned.1.call-done = f32[512,1024]{1,0:T(8,128)} async-done(((f32[2048,1024]{1,0:T(8,128)}), f32[512,1024]{1,0:T(8,128)}) %reduce-scatter.33.cloned.1.call-update) | async-done | bytes 2097168 | tf_op jit(solution)/shard_map/reduce_scatter | solution.py:208
  314.6 24.8 %all-gather.15.cloned.1.call-done = bf16[2048,1024]{1,0:T(8,128)(2,1)} async-done(((bf16[512,1024]{1,0:T(8,128)(2,1)}), bf16[2048,1024]{1,0:T(8,128)(2,1)}) %all-gather.15.cloned.1.call-update) | async-done | bytes 4194320 | tf_op jit(solution)/shard_map/all_gather | solution.py:204
  339.4 11.3 fusion.104
  350.8 25.4 %all-gather.17.cloned.1.call-done = bf16[2048,1024]{1,0:T(8,128)(2,1)} async-done(((bf16[512,1024]{1,0:T(8,128)(2,1)}), bf16[2048,1024]{1,0:T(8,128)(2,1)}) %all-gather.17.cloned.1.call-update) | async-done | bytes 4194320 | tf_op jit(solution)/shard_map/all_gather | solution.py:217
  376.2 12.8 convert_reduce_fusion
  391.0 6.9 fusion.105
  398.1 13.9 fusion.88
  412.7 57.0 %reduce-scatter.37.cloned.1.call-done = f32[512,1024]{1,0:T(8,128)} async-done(((f32[2048,1024]{1,0:T(8,128)}), f32[512,1024]{1,0:T(8,128)}) %reduce-scatter.37.cloned.1.call-update) | async-done | bytes 2097168 | tf_op jit(solution)/shard_map/reduce_scatter | solution.py:221
  471.9 72.0 %reduce-scatter.35.cloned.1.call-done = f32[512,1024]{1,0:T(8,128)} async-done(((f32[2048,1024]{1,0:T(8,128)}), f32[512,1024]{1,0:T(8,128)}) %reduce-scatter.35.cloned.1.call-update) | async-done | bytes 2097168 | tf_op jit(solution)/shard_map/reduce_scatter | solution.py:208
  543.9 5.9 fusion.93
  549.9 34.6 %all-gather.19.cloned.1.call-done = bf16[2048,1024]{1,0:T(8,128)(2,1)} async-done(((bf16[512,1024]{1,0:T(8,128)(2,1)}), bf16[2048,1024]{1,0:T(8,128)(2,1)}) %all-gather.19.cloned.1.call-update) | async-done | bytes 4194320 | tf_op jit(solution)/shard_map/all_gather | solution.py:217
  590.1 6.0 convert_bitcast_fusion
  596.2 4.3 fusion.26
  607.2 6.0 fusion.40
  633.8 7.0 fusion.106
  640.8 71.8 %reduce-scatter.39.cloned.1.call-done = f32[512,1024]{1,0:T(8,128)} async-done(((f32[2048,1024]{1,0:T(8,128)}), f32[512,1024]{1,0:T(8,128)}) %reduce-scatter.39.cloned.1.call-update) | async-done | bytes 2097168 | tf_op jit(solution)/shard_map/reduce_scatter | solution.py:221
  721.7 16.8 %all-gather.21.cloned.1.call-done = bf16[512,1024]{1,0:T(8,128)(2,1)} async-done(((bf16[128,1024]{1,0:T(8,128)(2,1)}), bf16[512,1024]{1,0:T(8,128)(2,1)}) %all-gather.21.cloned.1.call-update) | async-done | bytes 1048592 | tf_op jit(solution)/shard_map/all_gather | solution.py:191
  738.5 5.2 convert_reduce_fusion.1
  747.0 25.0 %reduce-scatter.41.cloned.1.call-done = bf16[128,1024]{1,0:T(8,128)(2,1)} async-done(((bf16[512,1024]{1,0:T(8,128)(2,1)}), bf16[128,1024]{1,0:T(8,128)(2,1)}) %reduce-scatter.41.cloned.1.call-update) | async-done | bytes 262160 | tf_op jit(solution)/shard_map/reduce_scatter | solution.py:195
  775.6 10.6 convolution_convert_fusion.2
  788.9 9.4 convolution_convert_fusion.3
  803.1 6.7 convolution_convert_fusion.7
  843.5 20.5 %reduce-scatter.67.cloned.1.call-done = bf16[128,1024]{1,0:T(8,128)(2,1)} async-done(((bf16[1024,1024]{1,0:T(8,128)(2,1)}), bf16[128,1024]{1,0:T(8,128)(2,1)}) %reduce-scatter.67.cloned.1.call-update) | async-done | bytes 262160
  865.9 69.3 %reduce-scatter.59.cloned.1.call-done = bf16[128,1024]{1,0:T(8,128)(2,1)} async-done(((bf16[1024,1024]{1,0:T(8,128)(2,1)}), bf16[128,1024]{1,0:T(8,128)(2,1)}) %reduce-scatter.59.cloned.1.call-update) | async-done | bytes 262160 | tf_op jit(solution)/shard_map/reduce_scatter | solution.py:467
  942.2 57.7 %reduce-scatter.65.cloned.1.call-done = bf16[128,256]{1,0:T(8,128)(2,1)} async-done(((bf16[1024,256]{1,0:T(8,128)(2,1)}), bf16[128,256]{1,0:T(8,128)(2,1)}) %reduce-scatter.65.cloned.1.call-update) | async-done | bytes 65552
  1001.5 62.7 %reduce-scatter.53.cloned.1.call-done = bf16[128,256]{1,0:T(8,128)(2,1)} async-done(((bf16[1024,256]{1,0:T(8,128)(2,1)}), bf16[128,256]{1,0:T(8,128)(2,1)}) %reduce-scatter.53.cloned.1.call-update) | async-done | bytes 65552 | tf_op jit(solution)/shard_map/reduce_scatter | solution.py:455
  1065.6 63.6 %reduce-scatter.55.cloned.1.call-done = bf16[128,256]{1,0:T(8,128)(2,1)} async-done(((bf16[1024,256]{1,0:T(8,128)(2,1)}), bf16[128,256]{1,0:T(8,128)(2,1)}) %reduce-scatter.55.cloned.1.call-update) | async-done | bytes 65552 | tf_op jit(solution)/shard_map/reduce_scatter | solution.py:458
  1130.7 63.4 %reduce-scatter.57.cloned.1.call-done = bf16[128,256]{1,0:T(8,128)(2,1)} async-done(((bf16[1024,256]{1,0:T(8,128)(2,1)}), bf16[128,256]{1,0:T(8,128)(2,1)}) %reduce-scatter.57.cloned.1.call-update) | async-done | bytes 65552 | tf_op jit(solution)/shard_map/reduce_scatter | solution.py:461
  1198.5 66.2 %reduce-scatter.63.cloned.1.call-done = bf16[128,1024]{1,0:T(8,128)(2,1)} async-done(((bf16[1024,1024]{1,0:T(8,128)(2,1)}), bf16[128,1024]{1,0:T(8,128)(2,1)}) %reduce-scatter.63.cloned.1.call-update) | async-done | bytes 262160
  1266.7 68.9 %reduce-scatter.51.cloned.1.call-done = bf16[128,1024]{1,0:T(8,128)(2,1)} async-done(((bf16[1024,1024]{1,0:T(8,128)(2,1)}), bf16[128,1024]{1,0:T(8,128)(2,1)}) %reduce-scatter.51.cloned.1.call-update) | async-done | bytes 262160 | tf_op jit(solution)/shard_map/reduce_scatter | solution.py:449
  1337.4 62.8 %reduce-scatter.61.cloned.1.call-done = bf16[128,256]{1,0:T(8,128)(2,1)} async-done(((bf16[1024,256]{1,0:T(8,128)(2,1)}), bf16[128,256]{1,0:T(8,128)(2,1)}) %reduce-scatter.61.cloned.1.call-update) | async-done | bytes 65552
  1401.9 62.7 %reduce-scatter.45.cloned.1.call-done = bf16[128,256]{1,0:T(8,128)(2,1)} async-done(((bf16[1024,256]{1,0:T(8,128)(2,1)}), bf16[128,256]{1,0:T(8,128)(2,1)}) %reduce-scatter.45.cloned.1.call-update) | async-done | bytes 65552 | tf_op jit(solution)/shard_map/reduce_scatter | solution.py:437
  1466.1 63.0 %reduce-scatter.47.cloned.1.call-done = bf16[128,256]{1,0:T(8,128)(2,1)} async-done(((bf16[1024,256]{1,0:T(8,128)(2,1)}), bf16[128,256]{1,0:T(8,128)(2,1)}) %reduce-scatter.47.cloned.1.call-update) | async-done | bytes 65552 | tf_op jit(solution)/shard_map/reduce_scatter | solution.py:440
  1530.5 62.6 %reduce-scatter.49.cloned.1.call-done = bf16[128,256]{1,0:T(8,128)(2,1)} async-done(((bf16[1024,256]{1,0:T(8,128)(2,1)}), bf16[128,256]{1,0:T(8,128)(2,1)}) %reduce-scatter.49.cloned.1.call-update) | async-done | bytes 65552 | tf_op jit(solution)/shard_map/reduce_scatter | solution.py:443
  1594.7 25.1 %reduce-scatter.43.cloned.1.call-done = bf16[128,1024]{1,0:T(8,128)(2,1)} async-done(((bf16[512,1024]{1,0:T(8,128)(2,1)}), bf16[128,1024]{1,0:T(8,128)(2,1)}) %reduce-scatter.43.cloned.1.call-update) | async-done | bytes 262160 | tf_op jit(solution)/shard_map/reduce_scatter | solution.py:195
  1621.0 40.8 %all-reduce = (f32[1024]{0:T(1024)}, f32[1024]{0:T(1024)}, f32[4096]{0:T(1024)}, f32[1024]{0:T(1024)}, f32[1024]{0:T(1024)}, /*index=5*/f32[1024]{0:T(1024)}, f32[4096]{0:T(1024)}, f32[1024]{0:T(1024)}) all-reduce(f32[1024]{0:T(1024)S(1)} %get-tuple-element.153, ...), channel_id=1, replica_groups=mesh['dp'=8,'tensor'=4] {'dp','tensor'}, use_global_device_ids=true, to_apply=%region_23.24 | all-reduce | flops 14336 | bytes 114688 | tf_op jit(solution)/shard_map/psum | solution.py:475
  (347 shorter events, 199.8 us)
Async XLA Ops:
  7.2 369.0 %copy-start = (bf16[1024,1024]{1,0:T(8,128)(2,1)S(1)}, bf16[1024,1024]{1,0:T(8,128)(2,1)}, u32[]{:S(2)}) copy-start(bf16[1024,1024]{1,0:T(8,128)(2,1)} %param.46) | copy-start | bytes 6291460
  7.2 24.6 %all-gather.9.cloned.1.call-start = ((), (), s32[]{:S(2)}) async-start(), calls=%async_computation.20 | async-start | bytes 1310720 | tf_op jit(solution)/shard_map/all_gather | solution.py:178
  12.2 60.8 %reduce-scatter.29.cloned.1.call-start = ((), (), s32[]{:S(2)}) async-start(), calls=%async_computation.21 | async-start | bytes 2621440 | tf_op jit(solution)/shard_map/reduce_scatter | solution.py:182
  39.6 33.4 %copy-start.14 = (bf16[128,1024]{1,0:T(8,128)(2,1)S(1)}, bf16[128,1024]{1,0:T(8,128)(2,1)}, u32[]{:S(2)}) copy-start(bf16[128,1024]{1,0:T(8,128)(2,1)} %param.25) | copy-start | bytes 786436
  41.4 34.2 %copy-start.60 = (bf16[1024]{0:T(1024)(128)(2,1)S(1)}, bf16[1024]{0:T(1024)(128)(2,1)}, u32[]{:S(2)}) copy-start(bf16[1024]{0:T(1024)(128)(2,1)} %param.35) | copy-start | bytes 6148
  41.4 51.0 %all-gather.11.cloned.1.call-start = ((), (), s32[]{:S(2)}) async-start(), calls=%async_computation.22 | async-start | bytes 1310720 | tf_op jit(solution)/shard_map/all_gather | solution.py:178
  41.5 54.3 %copy-start.50 = (f32[1024]{0:T(1024)}, f32[1024]{0:T(1024)S(1)}, u32[]{:S(2)}) copy-start(f32[1024]{0:T(1024)S(1)} %convert_element_type.273) | copy-start | bytes 12292
  74.3 57.4 %copy-start.7 = (f32[128,1024]{1,0:T(8,128)}, f32[128,1024]{1,0:T(8,128)S(1)}, u32[]{:S(2)}) copy-start(f32[128,1024]{1,0:T(8,128)S(1)} %get-tuple-element.174) | copy-start | bytes 1572868
  75.6 56.0 %reduce-scatter.31.cloned.1.call-start = ((), (), s32[]{:S(2)}) async-start(), calls=%async_computation.23 | async-start | bytes 2621440 | tf_op jit(solution)/shard_map/reduce_scatter | solution.py:182
  100.0 80.2 %all-gather.13.cloned.1.call-start = ((), (), s32[]{:S(2)}) async-start(), calls=%async_computation.24 | async-start | bytes 5242880 | tf_op jit(solution)/shard_map/all_gather | solution.py:204
  145.6 154.1 %reduce-scatter.33.cloned.1.call-start = ((), (), s32[]{:S(2)}) async-start(), calls=%async_computation.25 | async-start | bytes 10485760 | tf_op jit(solution)/shard_map/reduce_scatter | solution.py:208
  227.8 111.6 %all-gather.15.cloned.1.call-start = ((), (), s32[]{:S(2)}) async-start(), calls=%async_computation.26 | async-start | bytes 5242880 | tf_op jit(solution)/shard_map/all_gather | solution.py:204
  304.8 71.4 %all-gather.17.cloned.1.call-start = ((), (), s32[]{:S(2)}) async-start(), calls=%async_computation.28 | async-start | bytes 5242880 | tf_op jit(solution)/shard_map/all_gather | solution.py:217
  314.5 155.2 %reduce-scatter.37.cloned.1.call-start = ((), (), s32[]{:S(2)}) async-start(), calls=%async_computation.29 | async-start | bytes 10485760 | tf_op jit(solution)/shard_map/reduce_scatter | solution.py:221
  397.9 146.0 %reduce-scatter.35.cloned.1.call-start = ((), (), s32[]{:S(2)}) async-start(), calls=%async_computation.27 | async-start | bytes 10485760 | tf_op jit(solution)/shard_map/reduce_scatter | solution.py:208
  412.1 57.7 %copy-start.6 = (f32[512,1024]{1,0:T(8,128)S(1)}, f32[512,1024]{1,0:T(8,128)}, u32[]{:S(2)}) copy-start(f32[512,1024]{1,0:T(8,128)} %copy-done.5) | copy-start | bytes 6291460
  412.1 172.4 %all-gather.19.cloned.1.call-start = ((), (), s32[]{:S(2)}) async-start(), calls=%async_computation.30 | async-start | bytes 5242880 | tf_op jit(solution)/shard_map/all_gather | solution.py:217
  549.9 162.8 %reduce-scatter.39.cloned.1.call-start = ((), (), s32[]{:S(2)}) async-start(), calls=%async_computation.31 | async-start | bytes 10485760 | tf_op jit(solution)/shard_map/reduce_scatter | solution.py:221
  640.8 71.9 %copy-start.4 = (f32[512,1024]{1,0:T(8,128)S(1)}, f32[512,1024]{1,0:T(8,128)}, u32[]{:S(2)}) copy-start(f32[512,1024]{1,0:T(8,128)} %reshape.270) | copy-start | bytes 6291460
  640.8 97.7 %all-gather.21.cloned.1.call-start = ((), (), s32[]{:S(2)}) async-start(), calls=%async_computation.32 | async-start | bytes 1310720 | tf_op jit(solution)/shard_map/all_gather | solution.py:191
  721.6 50.4 %reduce-scatter.41.cloned.1.call-start = ((), (), s32[]{:S(2)}) async-start(), calls=%async_computation.33 | async-start | bytes 1310720 | tf_op jit(solution)/shard_map/reduce_scatter | solution.py:195
  744.7 27.4 %copy-start.8 = (f32[128,1024]{1,0:T(8,128)S(1)}, f32[128,1024]{1,0:T(8,128)}, u32[]{:S(2)}) copy-start(f32[128,1024]{1,0:T(8,128)} %copy-done.7) | copy-start | bytes 1572868
  744.7 27.4 %copy-start.51 = (f32[1024]{0:T(1024)S(1)}, f32[1024]{0:T(1024)}, u32[]{:S(2)}) copy-start(f32[1024]{0:T(1024)} %copy-done.50) | copy-start | bytes 12292
  744.7 27.4 %copy-start.58 = (f32[128]{0:T(128)S(1)}, f32[128]{0:T(128)}, u32[]{:S(2)}) copy-start(f32[128]{0:T(128)} %copy-done.57) | copy-start | bytes 1540
  744.7 28.5 %copy-start.69 = (f32[128]{0:T(128)S(1)}, f32[128]{0:T(128)}, u32[]{:S(2)}) copy-start(f32[128]{0:T(128)} %copy-done.68) | copy-start | bytes 1540
  747.0 76.3 %all-gather.23.cloned.1.call-start = ((), (), s32[]{:S(2)}) async-start(), calls=%async_computation.34 | async-start | bytes 1310720 | tf_op jit(solution)/shard_map/all_gather | solution.py:191
  775.4 88.5 %reduce-scatter.67.cloned.1.call-start = ((), (), s32[]{:S(2)}) async-start(), calls=%async_computation.47 | async-start | bytes 2359296
  788.8 146.4 %reduce-scatter.59.cloned.1.call-start = ((), (), s32[]{:S(2)}) async-start(), calls=%async_computation.43 | async-start | bytes 2359296 | tf_op jit(solution)/shard_map/reduce_scatter | solution.py:467
  798.3 201.5 %reduce-scatter.65.cloned.1.call-start = ((), (), s32[]{:S(2)}) async-start(), calls=%async_computation.46 | async-start | bytes 589824
  802.9 261.3 %reduce-scatter.53.cloned.1.call-start = ((), (), s32[]{:S(2)}) async-start(), calls=%async_computation.40 | async-start | bytes 589824 | tf_op jit(solution)/shard_map/reduce_scatter | solution.py:455
  811.1 318.2 %reduce-scatter.55.cloned.1.call-start = ((), (), s32[]{:S(2)}) async-start(), calls=%async_computation.41 | async-start | bytes 589824 | tf_op jit(solution)/shard_map/reduce_scatter | solution.py:458
  811.6 382.4 %reduce-scatter.57.cloned.1.call-start = ((), (), s32[]{:S(2)}) async-start(), calls=%async_computation.42 | async-start | bytes 589824 | tf_op jit(solution)/shard_map/reduce_scatter | solution.py:461
  812.4 452.4 %reduce-scatter.63.cloned.1.call-start = ((), (), s32[]{:S(2)}) async-start(), calls=%async_computation.45 | async-start | bytes 2359296
  818.3 517.3 %reduce-scatter.51.cloned.1.call-start = ((), (), s32[]{:S(2)}) async-start(), calls=%async_computation.39 | async-start | bytes 2359296 | tf_op jit(solution)/shard_map/reduce_scatter | solution.py:449
  822.5 577.7 %reduce-scatter.61.cloned.1.call-start = ((), (), s32[]{:S(2)}) async-start(), calls=%async_computation.44 | async-start | bytes 589824
  832.4 632.2 %reduce-scatter.45.cloned.1.call-start = ((), (), s32[]{:S(2)}) async-start(), calls=%async_computation.36 | async-start | bytes 589824 | tf_op jit(solution)/shard_map/reduce_scatter | solution.py:437
  838.5 690.5 %reduce-scatter.47.cloned.1.call-start = ((), (), s32[]{:S(2)}) async-start(), calls=%async_computation.37 | async-start | bytes 589824 | tf_op jit(solution)/shard_map/reduce_scatter | solution.py:440
  839.1 754.1 %reduce-scatter.49.cloned.1.call-start = ((), (), s32[]{:S(2)}) async-start(), calls=%async_computation.38 | async-start | bytes 589824 | tf_op jit(solution)/shard_map/reduce_scatter | solution.py:443
  839.7 780.1 %reduce-scatter.43.cloned.1.call-start = ((), (), s32[]{:S(2)}) async-start(), calls=%async_computation.35 | async-start | bytes 1310720 | tf_op jit(solution)/shard_map/reduce_scatter | solution.py:195
  843.2 93.9 %copy-start.13 = (f32[512,1024]{1,0:T(8,128)S(1)}, f32[512,1024]{1,0:T(8,128)}, u32[]{:S(2)}) copy-start(f32[512,1024]{1,0:T(8,128)} %get-tuple-element.178) | copy-start | bytes 6291460
  938.7 256.9 %copy-start.10 = (f32[128,4,1024]{2,1,0:T(4,128)S(1)}, f32[128,4,1024]{2,1,0:T(4,128)}, u32[]{:S(2)}) copy-start(f32[128,4,1024]{2,1,0:T(4,128)} %copy-done.9) | copy-start | bytes 6291460
  1198.2 421.6 %copy-start.15 = (bf16[128,1024]{1,0:T(8,128)(2,1)S(1)}, bf16[128,1024]{1,0:T(8,128)(2,1)}, u32[]{:S(2)}) copy-start(bf16[128,1024]{1,0:T(8,128)(2,1)} %param.25) | copy-start | bytes 786436
  1198.2 421.6 %copy-start.49 = (f32[1024]{0:T(1024)S(1)}, f32[1024]{0:T(1024)}, u32[]{:S(2)}) copy-start(f32[1024]{0:T(1024)} %copy-done.48) | copy-start | bytes 12292
  1198.2 421.6 %copy-start.56 = (f32[128]{0:T(128)S(1)}, f32[128]{0:T(128)}, u32[]{:S(2)}) copy-start(f32[128]{0:T(128)} %copy-done.55) | copy-start | bytes 1540
  1198.2 422.8 %copy-start.67 = (f32[128]{0:T(128)S(1)}, f32[128]{0:T(128)}, u32[]{:S(2)}) copy-start(f32[128]{0:T(128)} %copy-done.66) | copy-start | bytes 1540
  1198.2 422.8 %copy-start.54 = (f32[1024]{0:T(1024)S(1)}, f32[1024]{0:T(1024)}, u32[]{:S(2)}) copy-start(f32[1024]{0:T(1024)} %get-tuple-element.189) | copy-start | bytes 12292
  1198.2 463.6 %copy-start.30 = (f32[128,1024]{1,0:T(8,128)S(1)}, f32[128,1024]{1,0:T(8,128)}, u32[]{:S(2)}) copy-start(f32[128,1024]{1,0:T(8,128)} %get-tuple-element.168) | copy-start | bytes 1572868
  1265.9 397.8 %copy-start.1 = (bf16[1024,1024]{1,0:T(8,128)(2,1)S(1)}, bf16[1024,1024]{1,0:T(8,128)(2,1)}, u32[]{:S(2)}) copy-start(bf16[1024,1024]{1,0:T(8,128)(2,1)} %param.46) | copy-start | bytes 6291460
  (60 other events, 217.4 us)
Sparse Core Ops, SparseCore 0:
  12.3 19.4 all-gather.8
  41.6 31.4 reduce-scatter.28
  75.7 16.7 all-gather.10
  100.2 31.4 reduce-scatter.30
  145.7 34.4 all-gather.12
  227.9 71.7 reduce-scatter.32
  304.9 34.4 all-gather.14
  341.6 34.4 all-gather.16
  398.0 71.6 reduce-scatter.36
  472.2 71.6 reduce-scatter.34
  550.0 34.4 all-gather.18
  640.9 71.6 reduce-scatter.38
  721.7 16.7 all-gather.20
  747.1 24.8 reduce-scatter.40
  775.5 16.7 all-gather.22
  796.1 67.8 reduce-scatter.66
  868.3 66.8 reduce-scatter.58
  938.8 60.9 reduce-scatter.64
  1003.2 60.9 reduce-scatter.52
  1068.3 60.8 reduce-scatter.54
  1133.1 60.8 reduce-scatter.56
  1198.0 66.6 reduce-scatter.62
  1268.7 66.8 reduce-scatter.50
  1339.2 61.0 reduce-scatter.60
  1403.6 60.9 reduce-scatter.44
  1468.1 60.8 reduce-scatter.46
  1532.2 60.8 reduce-scatter.48
  1595.9 23.8 reduce-scatter.42
where the time goes:
time: 1680 us; the launch traced here: 1670 us
  waiting for transfers between devices  1270 us (76%)
  matrix products  168 us (10%)
  local copies, waits for them, and re-layouts  103 us (6%)
  other arithmetic  65 us (4%)
  blocking collectives  40.8 us (2%)
    unnamed x32, waiting for transfers between devices  210 us
    reduce_scatter x2, waiting for transfers between devices, inner_collect(): lax.psum_scatter(make_rows(jnp.int32(0), row_count * lax.axis_size('tenso...  143 us
    reduce_scatter x2, waiting for transfers between devices, inner_collect_grad(): lax.psum_scatter(make_rows(jnp.int32(0), row_count * lax.axis_size('tenso...  129 us
    reduce_scatter x1, waiting for transfers between devices, per_device(): lax.psum_scatter(inner_grads[6].astype(jnp.bfloat16), 'dp', scatter_dimen...  69.3 us
    reduce_scatter x1, waiting for transfers between devices, per_device(): lax.psum_scatter(outer_grads[6].astype(jnp.bfloat16), 'dp', scatter_dimen...  68.9 us
    reduce_scatter x1, waiting for transfers between devices, per_device(): lax.psum_scatter(inner_grads[2].astype(jnp.bfloat16), 'dp', scatter_dimen...  63.6 us
    reduce_scatter x1, waiting for transfers between devices, per_device(): lax.psum_scatter(inner_grads[3].astype(jnp.bfloat16), 'dp', scatter_dimen...  63.4 us
    reduce_scatter x1, waiting for transfers between devices, per_device(): lax.psum_scatter(outer_grads[2].astype(jnp.bfloat16), 'dp', scatter_dimen...  63 us
  transfers between devices with their start and end apart: 28, of which 27 were waited for; matrix products, arithmetic and copies ran while one was open for 8% of the time, Pallas kernels for 0%

commit v1 on v0

v1 whole, which is shorter than its diff:
```python
import functools

import jax
import jax.numpy as jnp
from jax import lax
from jax.experimental import pallas as pl
from jax.experimental.pallas import tpu as pltpu
from jax.sharding import PartitionSpec as P

HEAD_DIM = 64
PAIR = 2 * HEAD_DIM
SLOTS = 4
EPSILON = 1e-05
MASKED = -1e30
SCALE = HEAD_DIM ** (-0.5)
F32 = jnp.float32
BF16 = jnp.bfloat16


def norm_rows(values, norm_gain):
    return (
        values * lax.rsqrt(jnp.mean(values * values, axis=-1, keepdims=True) + EPSILON) * norm_gain
    )


def mm(left, right):
    return jnp.dot(left, right, preferred_element_type=F32)


def mm_t(left, right):
    return lax.dot_general(left, right, (((1,), (1,)), ((), ())), preferred_element_type=F32)


def t_mm(left, right):
    return lax.dot_general(left, right, (((0,), (0,)), ((), ())), preferred_element_type=F32)


def swap(values, axis, mask):
    size = lax.axis_size(axis)
    return lax.ppermute(values, axis, [(i, i ^ mask) for i in range(size)])


def bits_of(size):
    return [1 << i for i in range(size.bit_length() - 1)]


def stack_heads(pair):
    lane = lax.broadcasted_iota(jnp.int32, pair.shape, 1)
    low = (lane < HEAD_DIM).astype(F32).astype(BF16)
    high = (lane >= HEAD_DIM).astype(F32).astype(BF16)
    return jnp.concatenate([pair * low, pair * high], axis=0)


def split_heads(stacked):
    rows = stacked.shape[0] // 2
    lane = lax.broadcasted_iota(jnp.int32, (rows, stacked.shape[1]), 1)
    return jnp.where(lane < HEAD_DIM, stacked[:rows], stacked[rows:])


def softmax_of(query2, key, allowed):
    scores = jnp.where(allowed, mm_t(query2, key) * SCALE, MASKED)
    raised = jnp.exp(scores - jnp.max(scores, axis=-1, keepdims=True))
    return raised / jnp.sum(raised, axis=-1, keepdims=True)


def pair_forward(query, key, value, allowed):
    probs = softmax_of(stack_heads(query), key, allowed)
    return split_heads(mm(probs.astype(BF16), value)).astype(BF16)


def pair_backward(query, key, value, grad, allowed):
    query2 = stack_heads(query)
    grad2 = stack_heads(grad)
    probs = softmax_of(query2, key, allowed)
    grad_probs = mm_t(grad2, value)
    row_inner = jnp.sum(probs * grad_probs, axis=-1, keepdims=True)
    grad_scores = (probs * (grad_probs - row_inner)).astype(BF16)
    grad_query = split_heads(mm(grad_scores, key)) * SCALE
    grad_key = t_mm(grad_scores, query2) * SCALE
    grad_value = t_mm(probs.astype(BF16), grad2)
    return grad_query, grad_key, grad_value


def inner_allowed(rows):
    per = rows // SLOTS
    row = lax.broadcasted_iota(jnp.int32, (2 * rows, rows), 0) % rows
    col = lax.broadcasted_iota(jnp.int32, (2 * rows, rows), 1)
    return (row % per == col % per) & (col // per <= row // per)


def inner_forward_kernel(query_ref, key_ref, value_ref, context_ref):
    slots, per, width = query_ref.shape
    rows = slots * per
    allowed = inner_allowed(rows)
    for lane in range(0, width, PAIR):
        pick = lambda ref: ref[:, :, lane : lane + PAIR].reshape(rows, PAIR)
        context = pair_forward(pick(query_ref), pick(key_ref), pick(value_ref), allowed)
        context_ref[:, :, lane : lane + PAIR] = context.reshape(slots, per, PAIR)


def inner_backward_kernel(query_ref, key_ref, value_ref, grad_ref, out_ref):
    slots, per, width = query_ref.shape
    rows = slots * per
    allowed = inner_allowed(rows)
    for lane in range(0, width, PAIR):
        pick = lambda ref: ref[:, :, lane : lane + PAIR].reshape(rows, PAIR)
        grads = pair_backward(
            pick(query_ref), pick(key_ref), pick(value_ref), pick(grad_ref), allowed
        )
        for which, grad in enumerate(grads):
            start = which * width + lane
            out_ref[:, :, start : start + PAIR] = grad.astype(BF16).reshape(slots, per, PAIR)


def inner_specs(frames, width, per):
    piece = lambda which: pl.BlockSpec((SLOTS, per, width), lambda i: (0, i, which))
    return [piece(0), piece(1), piece(2)], (frames // per,)


def inner_attend(projected):
    rows, triple = projected.shape
    frames, width = rows // SLOTS, triple // 3
    per = min(32, frames)
    shaped = projected.reshape(SLOTS, frames, triple)
    specs, grid = inner_specs(frames, width, per)
    context = pl.pallas_call(
        inner_forward_kernel,
        grid=grid,
        in_specs=specs,
        out_specs=pl.BlockSpec((SLOTS, per, width), lambda i: (0, i, 0)),
        out_shape=jax.ShapeDtypeStruct((SLOTS, frames, width), BF16),
        name="inner_attend",
    )(shaped, shaped, shaped)
    return context.reshape(rows, width)


def inner_attend_back(projected, grad_context):
    rows, triple = projected.shape
    frames, width = rows // SLOTS, triple // 3
    per = min(32, frames)
    shaped = projected.reshape(SLOTS, frames, triple)
    specs, grid = inner_specs(frames, width, per)
    grads = pl.pallas_call(
        inner_backward_kernel,
        grid=grid,
        in_specs=specs + [pl.BlockSpec((SLOTS, per, width), lambda i: (0, i, 0))],
        out_specs=pl.BlockSpec((SLOTS, per, triple), lambda i: (0, i, 0)),
        out_shape=jax.ShapeDtypeStruct((SLOTS, frames, triple), BF16),
        name="inner_attend_back",
    )(shaped, shaped, shaped, grad_context.reshape(SLOTS, frames, width))
    return grads.reshape(rows, triple)


def outer_allowed(first, key_pos, rows):
    length = key_pos.shape[1]
    row = lax.broadcasted_iota(jnp.int32, (2 * rows, length), 0) % rows
    return key_pos <= row + first


def outer_forward_kernel(first_ref, key_pos_ref, query_ref, key_ref, value_ref, context_ref):
    allowed = outer_allowed(first_ref[pl.program_id(1)], key_pos_ref[...], query_ref.shape[0])
    context_ref[...] = pair_forward(query_ref[...], key_ref[...], value_ref[...], allowed)


def outer_backward_kernel(
    first_ref,
    key_pos_ref,
    query_ref,
    key_ref,
    value_ref,
    grad_ref,
    grad_query_ref,
    grad_key_ref,
    grad_value_ref,
    key_total,
    value_total,
):
    step = pl.program_id(1)
    allowed = outer_allowed(first_ref[step], key_pos_ref[...], query_ref.shape[0])
    grad_query, grad_key, grad_value = pair_backward(
        query_ref[...], key_ref[...], value_ref[...], grad_ref[...], allowed
    )
    grad_query_ref[...] = grad_query.astype(BF16)

    @pl.when(step == 0)
    def _():
        key_total[...] = grad_key
        value_total[...] = grad_value

    @pl.when(step > 0)
    def _():
        key_total[...] += grad_key
        value_total[...] += grad_value

    @pl.when(step == pl.num_programs(1) - 1)
    def _():
        grad_key_ref[...] = key_total[...].astype(BF16)
        grad_value_ref[...] = value_total[...].astype(BF16)


def outer_attend_specs(length, block, pairs):
    return [
        pl.BlockSpec((1, length), lambda p, i, first: (0, 0)),
        pl.BlockSpec((block, PAIR), lambda p, i, first: (i, p)),
        pl.BlockSpec((length, PAIR), lambda p, i, first: (0, pairs + p)),
        pl.BlockSpec((length, PAIR), lambda p, i, first: (0, 2 * pairs + p)),
    ]


def outer_attend(projected, firsts, key_pos):
    length, triple = projected.shape
    width = triple // 3
    pairs = width // PAIR
    block = length // firsts.shape[0]
    return pl.pallas_call(
        outer_forward_kernel,
        grid_spec=pltpu.PrefetchScalarGridSpec(
            num_scalar_prefetch=1,
            grid=(pairs, length // block),
            in_specs=outer_attend_specs(length, block, pairs),
            out_specs=pl.BlockSpec((block, PAIR), lambda p, i, first: (i, p)),
        ),
        out_shape=jax.ShapeDtypeStruct((length, width), BF16),
        name="outer_attend",
    )(firsts, key_pos, projected, projected, projected)


def outer_attend_back(projected, grad_context, firsts, key_pos):
    length, triple = projected.shape
    width = triple // 3
    pairs = width // PAIR
    block = length // firsts.shape[0]
    by_block = pl.BlockSpec((block, PAIR), lambda p, i, first: (i, p))
    by_pair = pl.BlockSpec((length, PAIR), lambda p, i, first: (0, p))
    whole = jax.ShapeDtypeStruct((length, width), BF16)
    return pl.pallas_call(
        outer_backward_kernel,
        grid_spec=pltpu.PrefetchScalarGridSpec(
            num_scalar_prefetch=1,
            grid=(pairs, length // block),
            in_specs=outer_attend_specs(length, block, pairs) + [by_block],
            out_specs=[by_block, by_pair, by_pair],
            scratch_shapes=[pltpu.VMEM((length, PAIR), F32), pltpu.VMEM((length, PAIR), F32)],
        ),
        out_shape=[whole, whole, whole],
        name="outer_attend_back",
    )(firsts, key_pos, projected, projected, projected, grad_context)


def relative_order():
    size = lax.axis_size("tensor")
    return [k for k in range(size) if not k & 1] + [k for k in range(size) if k & 1]


def gather_rows(values):
    have = {0: values}
    for bit in reversed(bits_of(lax.axis_size("tensor"))):
        have.update({k | bit: swap(v, "tensor", bit) for k, v in list(have.items())})
    return jnp.concatenate([have[k] for k in relative_order()], axis=0)


def reduce_rows(partial_rows):
    order = relative_order()
    rows = partial_rows.shape[0] // len(order)
    have = {k: partial_rows[i * rows : (i + 1) * rows] for i, k in enumerate(order)}
    for bit in bits_of(lax.axis_size("tensor")):
        moved = {
            k: swap(v.astype(BF16), "tensor", bit) for k, v in have.items() if k & bit
        }
        have = {k: v + moved[k | bit].astype(F32) for k, v in have.items() if not k & bit}
    return have[0]


def by_own_bit(first, second, axis, mask):
    mine = (lax.axis_index(axis) & mask) != 0
    return jnp.where(mine, second, first), jnp.where(mine, first, second)


def half_columns(values, axis, mask):
    half = values.shape[1] // 2
    mine = ((lax.axis_index(axis) & mask) != 0).astype(jnp.int32)
    keep = lax.dynamic_slice_in_dim(values, mine * half, half, 1)
    send = lax.dynamic_slice_in_dim(values, (1 - mine) * half, half, 1)
    return keep, send


def order_columns(values, bits):
    count = lax.axis_size("dp")
    block = values.shape[1] // count
    places = []
    for place in range(count):
        index = 0
        for level, bit in enumerate(bits):
            if place >> (len(bits) - 1 - level) & 1:
                index |= bit
        places.append(index)
    return jnp.concatenate([values[:, i * block : (i + 1) * block] for i in places], axis=1)


def scatter_columns(total, bits):
    for bit in bits:
        keep, send = half_columns(total, "dp", bit)
        total = keep + swap(send.astype(BF16), "dp", bit).astype(F32)
    return total


def sum_all(vector):
    for axis in ("dp", "tensor"):
        for bit in bits_of(lax.axis_size(axis)):
            vector = vector + swap(vector, axis, bit)
    return vector


def gather_over_dp(piece):
    rows, width = piece.shape
    have = piece[None]
    for bit in reversed(bits_of(lax.axis_size("dp"))):
        other = swap(have, "dp", bit)
        mine = (lax.axis_index("dp") & bit) != 0
        low = jnp.where(mine, other, have)
        high = jnp.where(mine, have, other)
        have = jnp.stack([low, high], axis=1).reshape(-1, rows, width)
    return have


def gather_weights(shards):
    count = lax.axis_size("dp")
    size = lax.axis_size("tensor")
    here = lax.axis_index("dp")
    cut = [
        lax.dynamic_slice_in_dim(a, here * (a.shape[0] // count), a.shape[0] // count, 0)
        for a in shards
    ]
    groups = {}
    for i, a in enumerate(shards):
        groups.setdefault(a.shape[1], []).append(i)
    have = {0: list(shards)}
    for mask in range(2, size, 2):
        arrays = [None] * len(shards)
        for members in groups.values():
            pack = jnp.concatenate([cut[i] for i in members], axis=0)
            whole = gather_over_dp(swap(pack, "tensor", mask))
            start = 0
            for i in members:
                rows = cut[i].shape[0]
                arrays[i] = whole[:, start : start + rows].reshape(shards[i].shape)
                start += rows
        have[mask] = arrays
    for mask in range(0, size, 2):
        have[mask | 1] = [swap(a, "tensor", 1) for a in have[mask]]
    return have


def outer_forward(rows_in, weights, firsts, key_pos):
    gain_attn, w_qkv, w_merge, gain_mlp, w_up, up_bias, w_down, down_bias = weights
    gathered = gather_rows(norm_rows(rows_in, gain_attn).astype(BF16))
    projected = mm(gathered, w_qkv).astype(BF16)
    context = outer_attend(projected, firsts, key_pos)
    middle = rows_in + reduce_rows(mm(context, w_merge))
    gathered_mlp = gather_rows(norm_rows(middle, gain_mlp).astype(BF16))
    hidden_pre = mm(gathered_mlp, w_up) + up_bias
    hidden_low = jax.nn.gelu(hidden_pre).astype(BF16)
    output = middle + reduce_rows(mm(hidden_low, w_down)) + down_bias
    stored = (rows_in, middle, gathered, projected, context, gathered_mlp, hidden_pre, hidden_low)
    return output, stored


def outer_backward(grad_output, weights, stored, firsts, key_pos):
    gain_attn, w_qkv, w_merge, gain_mlp, w_up, up_bias, w_down, down_bias = weights
    rows_in, middle, gathered, projected, context, gathered_mlp, hidden_pre, hidden_low = stored
    bits = bits_of(lax.axis_size("dp"))
    grad_offset = jnp.sum(grad_output, axis=0)
    grad_full = gather_rows(grad_output.astype(BF16))
    grad_hidden = mm_t(grad_full, w_down)
    grad_pre = jax.vjp(jax.nn.gelu, hidden_pre)[1](grad_hidden)[0].astype(BF16)
    grad_down = scatter_columns(t_mm(hidden_low, order_columns(grad_full, bits)), bits)
    grad_shift = jnp.sum(grad_pre, axis=0, dtype=F32)
    grad_up = scatter_columns(t_mm(grad_pre, order_columns(gathered_mlp, bits)), bits)
    grad_normed_mlp = reduce_rows(mm_t(grad_pre, w_up))
    grad_middle_norm, grad_scale = jax.vjp(norm_rows, middle, gain_mlp)[1](grad_normed_mlp)
    grad_middle = grad_output + grad_middle_norm
    grad_branch = gather_rows(grad_middle.astype(BF16))
    grad_merge = scatter_columns(t_mm(context, order_columns(grad_branch, bits)), bits)
    grad_context = mm_t(grad_branch, w_merge).astype(BF16)
    grad_joined = jnp.concatenate(
        outer_attend_back(projected, grad_context, firsts, key_pos), axis=1
    )
    grad_qkv = scatter_columns(t_mm(grad_joined, order_columns(gathered, bits)), bits)
    grad_normed = reduce_rows(mm_t(grad_joined, w_qkv))
    grad_rows_norm, grad_gain = jax.vjp(norm_rows, rows_in, gain_attn)[1](grad_normed)
    grads = (grad_gain, grad_qkv, grad_merge, grad_scale, grad_up, grad_shift, grad_down, grad_offset)
    return grad_middle + grad_rows_norm, grads


def scatter_shards(own, send, bits):
    del send
    have = own
    for bit in bits_of(lax.axis_size("tensor")):
        moved = {k: swap(v.astype(BF16), "tensor", bit) for k, v in have.items() if k & bit}
        have = {k: v + moved[k | bit].astype(F32) for k, v in have.items() if not k & bit}
    return scatter_columns(have[0], bits)


def inner_block(sequence, grad_rows, small, full):
    gain_attn, gain_mlp, up_bias, down_bias = small
    keys = sorted(full)
    bits = bits_of(lax.axis_size("dp"))
    width = full[0][1].shape[0]
    w_qkv = jnp.concatenate(
        [full[k][0][:, i * width : (i + 1) * width] for i in range(3) for k in keys], axis=1
    )
    w_merge = jnp.concatenate([full[k][1] for k in keys], axis=0)
    normed = norm_rows(sequence, gain_attn).astype(BF16)
    projected = mm(normed, w_qkv).astype(BF16)
    context = inner_attend(projected)
    middle = sequence + mm(context, w_merge)
    normed_mlp = norm_rows(middle, gain_mlp).astype(BF16)
    hidden_pre = {k: mm(normed_mlp, full[k][2]) + up_bias[k] for k in keys}
    hidden_low = {k: jax.nn.gelu(v).astype(BF16) for k, v in hidden_pre.items()}
    output = middle + sum(mm(hidden_low[k], full[k][3]) for k in keys) + down_bias

    grad_offset = jnp.sum(grad_rows, axis=0)
    grad_low = grad_rows.astype(BF16)
    ordered = order_columns(grad_low, bits)
    grad_down = scatter_shards({k: t_mm(hidden_low[k], ordered) for k in keys}, None, bits)
    grad_hidden = {k: mm_t(grad_low, full[k][3]) for k in keys}
    grad_pre = {
        k: jax.vjp(jax.nn.gelu, hidden_pre[k])[1](grad_hidden[k])[0].astype(BF16) for k in keys
    }
    grad_shift = {k: jnp.sum(grad_pre[k], axis=0, dtype=F32) for k in keys}
    ordered = order_columns(normed_mlp, bits)
    grad_up = scatter_shards({k: t_mm(grad_pre[k], ordered) for k in keys}, None, bits)
    grad_normed_mlp = sum(mm_t(grad_pre[k], full[k][2]) for k in keys)
    grad_middle_norm, grad_scale = jax.vjp(norm_rows, middle, gain_mlp)[1](grad_normed_mlp)
    grad_middle = grad_rows + grad_middle_norm
    grad_branch = grad_middle.astype(BF16)
    ordered = order_columns(grad_branch, bits)
    grad_merge = scatter_shards(
        {k: t_mm(context[:, i * width : (i + 1) * width], ordered) for i, k in enumerate(keys)},
        None,
        bits,
    )
    grad_context = mm_t(grad_branch, w_merge).astype(BF16)
    grad_joined = inner_attend_back(projected, grad_context)
    ordered = order_columns(normed, bits)
    whole = width * len(keys)

    def joined_of(i):
        return jnp.concatenate(
            [grad_joined[:, j * whole + i * width : j * whole + (i + 1) * width] for j in range(3)],
            axis=1,
        )

    grad_qkv = scatter_shards(
        {k: t_mm(joined_of(i), ordered) for i, k in enumerate(keys)}, None, bits
    )
    grad_normed = mm_t(grad_joined, w_qkv)
    grad_rows_norm, grad_gain = jax.vjp(norm_rows, sequence, gain_attn)[1](grad_normed)
    grads = (grad_gain, grad_qkv, grad_merge, grad_scale, grad_up, grad_shift, grad_down, grad_offset)
    return output, grad_middle + grad_rows_norm, grads


def place_columns(values, total, which):
    return lax.dynamic_update_slice(
        jnp.zeros((total,), F32), values, (which * values.shape[0],)
    )


def matrix_outputs(grads):
    grad_gain, grad_qkv, grad_merge, grad_scale, grad_up, grad_shift, grad_down, grad_offset = grads
    width = grad_qkv.shape[0] // 3
    turned = grad_qkv.T
    return (
        turned[:, :width],
        turned[:, width : 2 * width],
        turned[:, 2 * width :],
        grad_merge,
        grad_up.T,
        grad_down,
    )


def per_device(
    frames_in,
    codes_in,
    lengths,
    outer_gain,
    outer_query,
    outer_key,
    outer_value,
    outer_merge,
    outer_scale,
    outer_up,
    outer_shift,
    outer_down,
    outer_offset,
    inner_gain,
    inner_query,
    inner_key,
    inner_value,
    inner_merge,
    inner_scale,
    inner_up,
    inner_shift,
    inner_down,
    inner_offset,
    cot_global,
    cot_local,
):
    rows, dim = frames_in.shape
    size = lax.axis_size("tensor")
    here = lax.axis_index("tensor")
    hidden = inner_up.shape[1]
    order = relative_order()
    firsts = jnp.stack([(here ^ k) * rows for k in order]).astype(jnp.int32)
    key_pos = (firsts[:, None] + jnp.arange(rows, dtype=jnp.int32)[None, :]).reshape(1, -1)
    positions = here * rows + jnp.arange(rows, dtype=jnp.int32)
    valid_rows = (positions < lengths[0]).astype(F32)

    full = gather_weights(
        [
            jnp.concatenate([inner_query, inner_key, inner_value], axis=1),
            inner_merge,
            inner_up,
            inner_down,
        ]
    )
    all_shift = lax.all_gather(inner_shift, "tensor", axis=0, tiled=False)
    shift_of = {
        k: lax.dynamic_index_in_dim(all_shift, here ^ k, 0, keepdims=False).astype(F32)
        for k in range(size)
    }

    outer_weights = (
        outer_gain.astype(F32),
        jnp.concatenate([outer_query, outer_key, outer_value], axis=1),
        outer_merge,
        outer_scale.astype(F32),
        outer_up,
        outer_shift.astype(F32),
        outer_down,
        outer_offset.astype(F32),
    )
    global_rows, outer_stored = outer_forward(
        frames_in.astype(F32), outer_weights, firsts, key_pos
    )
    sequence = jnp.concatenate(
        [global_rows[None], jnp.transpose(codes_in, (1, 0, 2)).astype(F32)], axis=0
    ).reshape(SLOTS * rows, dim)
    grad_local = (
        jnp.transpose(cot_local, (1, 0, 2)).astype(F32) * valid_rows[None, :, None]
    ).reshape(SLOTS * rows, dim)
    small = (
        inner_gain.astype(F32),
        inner_scale.astype(F32),
        shift_of,
        inner_offset.astype(F32),
    )
    local_rows, grad_sequence, inner_grads = inner_block(sequence, grad_local, small, full)
    grad_sequence = grad_sequence.reshape(SLOTS, rows, dim)
    grad_global = cot_global.astype(F32) * valid_rows[:, None] + grad_sequence[0]
    grad_frames, outer_grads = outer_backward(
        grad_global, outer_weights, outer_stored, firsts, key_pos
    )
    inner_shift_full = jnp.zeros((size, hidden), F32)
    for k in range(size):
        inner_shift_full = lax.dynamic_update_slice(
            inner_shift_full, inner_grads[5][k][None], (here ^ k, 0)
        )
    pieces = [
        outer_grads[0],
        outer_grads[3],
        outer_grads[7],
        place_columns(outer_grads[5], hidden * size, here),
        inner_grads[0],
        inner_grads[3],
        inner_grads[7],
        inner_shift_full.reshape(-1),
    ]
    summed = sum_all(jnp.concatenate(pieces).reshape(-1, 128)).reshape(-1)
    vectors = []
    start = 0
    for piece in pieces:
        vectors.append(summed[start : start + piece.shape[0]])
        start += piece.shape[0]
    outer_mats = matrix_outputs(outer_grads)
    inner_mats = matrix_outputs(inner_grads)
    local_out = jnp.transpose(local_rows.reshape(SLOTS, rows, dim), (1, 0, 2))
    return (
        global_rows * valid_rows[:, None],
        local_out * valid_rows[:, None, None],
        grad_frames,
        jnp.transpose(grad_sequence[1:], (1, 0, 2)),
        vectors[0],
        *outer_mats[:4],
        vectors[1],
        outer_mats[4],
        vectors[3],
        outer_mats[5],
        vectors[2],
        vectors[4],
        *inner_mats[:4],
        vectors[5],
        inner_mats[4],
        vectors[7],
        inner_mats[5],
        vectors[6],
    )


def solution(mesh):
    in_specs = (
        P(("dp", "tensor"), None),
        P(("dp", "tensor"), None, None),
        P("dp"),
        P(),
        P(None, "tensor"),
        P(None, "tensor"),
        P(None, "tensor"),
        P("tensor", None),
        P(),
        P(None, "tensor"),
        P("tensor"),
        P("tensor", None),
        P(),
        P(),
        P(None, "tensor"),
        P(None, "tensor"),
        P(None, "tensor"),
        P("tensor", None),
        P(),
        P(None, "tensor"),
        P("tensor"),
        P("tensor", None),
        P(),
        P(("dp", "tensor"), None),
        P(("dp", "tensor"), None, None),
    )
    out_specs = (
        P(("dp", "tensor"), None),
        P(("dp", "tensor"), None, None),
        P(("dp", "tensor"), None),
        P(("dp", "tensor"), None, None),
        P(),
        P("dp", "tensor"),
        P("dp", "tensor"),
        P("dp", "tensor"),
        P("tensor", "dp"),
        P(),
        P("dp", "tensor"),
        P(),
        P("tensor", "dp"),
        P(),
        P(),
        P("dp", "tensor"),
        P("dp", "tensor"),
        P("dp", "tensor"),
        P("tensor", "dp"),
        P(),
        P("dp", "tensor"),
        P(),
        P("tensor", "dp"),
        P(),
    )
    return jax.shard_map(
        per_device, mesh=mesh, in_specs=in_specs, out_specs=out_specs, check_vma=False
    )
```

time: 1680 us -> 760 us (0.45)
  waiting for transfers between devices: 1270 us -> 366 us
  starting transfers between devices: 2.58 us -> 60.6 us
  Pallas kernels: 0 us -> 43.3 us
  local copies, waits for them, and re-layouts: 103 us -> 62.8 us
  blocking collectives: 40.8 us -> 5.56 us
    reduce_scatter x16 -> x0, waiting for transfers between devices: 899 us -> none  [the longest x2 143 us: inner_collect(): lax.psum_scatter(make_rows(jnp.int32(0), row_count * lax.axis_size('tenso...]
    ppermute x0 -> x81, waiting for transfers between devices: none -> 366 us  [swap(): return lax.ppermute(values, axis, [(i, i ^ mask) for i in range(size)])]
    unnamed x32 -> x0, waiting for transfers between devices: 210 us -> none
    all_gather x8 -> x0, waiting for transfers between devices: 166 us -> none  [the longest x2 60 us: inner_spread_grad(): return lax.all_gather(values, 'tensor', axis=0, tiled=True)]
    ppermute x0 -> x81, starting transfers between devices: none -> 60.6 us  [swap(): return lax.ppermute(values, axis, [(i, i ^ mask) for i in range(size)])]
    pallas_call x0 -> x4, Pallas kernels: none -> 43.3 us  [the longest x1 18.1 us: inner_attend_back(): pl.pallas_call(inner_backward_kernel, grid=grid, in_specs=specs + [pl.Blo...]
    psum x1 -> x0, blocking collectives: 40.8 us -> none  [per_device(): lax.psum((outer_grads[0], outer_grads[5], place_columns(outer_grads[7]),...]
    convert_element_type x32 -> x21, other arithmetic: 37.6 us -> 12.1 us  [the longest x1 2.45 us: per_device(): jnp.transpose(codes_in, (1, 0, 2)).astype(F32)]
  transfers between devices with their start and end apart: 28 -> 81, of which waited for: 27 -> 35; matrix products, arithmetic and copies ran while one was open for 8% -> 31% of each run, Pallas kernels for 0% -> 3%
where the time goes in v1:
time: 760 us; the launch traced here: 754 us
  waiting for transfers between devices  366 us (48%)
  matrix products  156 us (21%)
  local copies, waits for them, and re-layouts  62.8 us (8%)
  starting transfers between devices  60.6 us (8%)
  other arithmetic  55.3 us (7%)
  Pallas kernels  43.3 us (6%)
    ppermute x81, waiting for transfers between devices, swap(): return lax.ppermute(values, axis, [(i, i ^ mask) for i in range(size)])  366 us
    ppermute x81, starting transfers between devices, swap(): return lax.ppermute(values, axis, [(i, i ^ mask) for i in range(size)])  60.6 us
    dot_general x14, matrix products, mm_t(): lax.dot_general(left, right, (((1,), (1,)), ((), ())), preferred_element_...  58.2 us
    dot_general x20, matrix products, t_mm(): lax.dot_general(left, right, (((0,), (0,)), ((), ())), preferred_element_...  52.4 us
    dot_general x14, matrix products, mm(): return jnp.dot(left, right, preferred_element_type=F32)  45.4 us
    unnamed x352, local copies, waits for them, and re-layouts  36.8 us
    pallas_call x1, Pallas kernels, inner_attend_back(): pl.pallas_call(inner_backward_kernel, grid=grid, in_specs=specs + [pl.Blo...  18.1 us
  transfers between devices with their start and end apart: 81, of which 35 were waited for; matrix products, arithmetic and copies ran while one was open for 31% of the time, Pallas kernels for 3%

profile of v1, /device:TPU:0, one launch (start us, length us, event | category | flops | bytes accessed | tf_op | source)
XLA Modules:
  0.0 754.4 jit_solution(2134952175525530946)
XLA Ops:
  22.1 5.6 all-gather
  46.0 7.7 %collective-permute-done.14 = bf16[1,128,768]{2,1,0:T(8,128)(2,1)S(1)} collective-permute-done((bf16[1,128,768]{2,1,0:T(8,128)(2,1)}, bf16[1,128,768]{2,1,0:T(8,128)(2,1)S(1)}, u32[]{:S(2)}, u32[]{:S(2)}) %collective-permute-start.14) | collective-permute-done | bytes 196640 | tf_op jit(solution)/shard_map/ppermute | solution.py:40
  59.1 8.0 %outer_attend.1 = bf16[512,256]{1,0:T(8,128)(2,1)} custom-call(s32[4]{0:T(128)} %copy-done.87, s32[1,512]{1,0:T(1,128)} %bitcast.246, bf16[512,768]{1,0:T(8,128)(2,1)} %convolution_convert_fusion.8.query_ref.key_ref.value_ref, bf16[512,768]{1,0:T(8,128)(2,1)} %convolution_convert_fusion.8.query_ref.key_ref.value_ref, ...), custom_call_target="tpu_custom_call" | custom-call | tf_op jit(solution)/shard_map/outer_attend/pallas_call | solution.py:215
  73.7 6.0 collective-permute-done.5
  80.1 7.2 collective-permute-done.15
  87.5 20.9 %collective-permute-done.20 = bf16[1,288,1024]{2,1,0:T(8,128)(2,1)S(1)} collective-permute-done((bf16[1,288,1024]{2,1,0:T(8,128)(2,1)}, bf16[1,288,1024]{2,1,0:T(8,128)(2,1)S(1)}, u32[]{:S(2)}, u32[]{:S(2)}) %collective-permute-start.20) | collective-permute-done | bytes 589856 | tf_op jit(solution)/shard_map/ppermute | solution.py:40
  115.3 14.9 %collective-permute-done.16 = bf16[4,128,768]{2,1,0:T(8,128)(2,1)S(1)} collective-permute-done((bf16[4,128,768]{2,1,0:T(8,128)(2,1)S(1)}, bf16[4,128,768]{2,1,0:T(8,128)(2,1)S(1)}, u32[]{:S(2)}, u32[]{:S(2)}) %collective-permute-start.16) | collective-permute-done | bytes 786464 | tf_op jit(solution)/shard_map/ppermute | solution.py:40
  134.4 6.5 collective-permute-done.11
  143.6 18.6 %collective-permute-done.21 = bf16[2,288,1024]{2,1,0:T(8,128)(2,1)S(1)} collective-permute-done((bf16[2,288,1024]{2,1,0:T(8,128)(2,1)S(1)}, bf16[2,288,1024]{2,1,0:T(8,128)(2,1)S(1)}, u32[]{:S(2)}, u32[]{:S(2)}) %collective-permute-start.21) | collective-permute-done | bytes 1179680 | tf_op jit(solution)/shard_map/ppermute | solution.py:40
  167.4 47.6 %collective-permute-done.22 = bf16[4,288,1024]{2,1,0:T(8,128)(2,1)S(1)} collective-permute-done((bf16[4,288,1024]{2,1,0:T(8,128)(2,1)S(1)}, bf16[4,288,1024]{2,1,0:T(8,128)(2,1)S(1)}, u32[]{:S(2)}, u32[]{:S(2)}) %collective-permute-start.22) | collective-permute-done | bytes 2359328 | tf_op jit(solution)/shard_map/ppermute | solution.py:40
  217.3 4.8 convolution_convert_fusion
  222.2 6.8 inner_attend.1
  228.9 5.0 fusion.122
  241.7 5.5 convert_reduce_fusion.3
  252.0 4.9 convert_reduce_fusion.1
  257.0 4.6 fusion.140
  261.7 4.6 fusion.138
  272.5 4.8 fusion.106
  277.4 4.2 convolution_convert_fusion.2
  281.5 5.2 convert_reduce_fusion.2
  292.9 4.6 fusion.110
  297.5 4.6 fusion.107
  302.1 4.6 fusion.108
  309.6 4.8 convert_reduce_fusion
  320.3 4.6 convolution_convert_fusion.7
  324.9 18.1 %inner_attend_back.1 = bf16[4,128,3072]{2,1,0:T(8,128)(2,1)} custom-call(bf16[4,128,3072]{2,1,0:T(8,128)(2,1)} %bitcast.219, bf16[4,128,3072]{2,1,0:T(8,128)(2,1)} %bitcast.220, bf16[4,128,3072]{2,1,0:T(8,128)(2,1)} %bitcast.221, bf16[4,128,1024]{2,1,0:T(8,128)(2,1)} %bitcast.241), custom_call_target="tpu_custom_call" | custom-call | tf_op jit(solution)/shard_map/inner_attend_back/pallas_call | solution.py:143
  342.9 8.2 %multiply_reduce_fusion.1 = (f32[1024]{0:T(1024)S(1)}, f32[512]{0:T(512)S(1)}, f32[512,1024]{1,0:T(8,128)S(1)}) fusion(f32[4,128,1024]{2,1,0:T(8,128)} %copy-done.2, f32[512]{0:T(512)S(1)} %bitcast_rsqrt_fusion, f32[1024]{0:T(1024)S(1)} %convert_element_type.468, bf16[512,3072]{1,0:T(8,128)(2,1)} %bitcast.224, bf16[1024,3072]{1,0:T(8,128)(2,1)} %copy-done.80), kind=kOutput, calls=%fused_computation.82 | convolution fusion | flops 3224369664 | bytes 13643776 | tf_op jit(solution)/shard_map/dot_general | solution.py:31
  360.4 4.3 convolution_convert_fusion.1
  379.2 4.2 fusion.38
  399.9 10.6 %collective-permute-done.65 = bf16[256,1024]{1,0:T(8,128)(2,1)S(1)} collective-permute-done((bf16[256,1024]{1,0:T(8,128)(2,1)S(1)}, bf16[256,1024]{1,0:T(8,128)(2,1)S(1)}, u32[]{:S(2)}, u32[]{:S(2)}) %collective-permute-start.65) | collective-permute-done | bytes 524320 | tf_op jit(solution)/shard_map/ppermute | solution.py:40
  420.9 4.5 collective-permute-done.67
  432.1 10.5 %collective-permute-done.51 = bf16[1024,512]{1,0:T(8,128)(2,1)S(1)} collective-permute-done((bf16[1024,512]{1,0:T(8,128)(2,1)S(1)}, bf16[1024,512]{1,0:T(8,128)(2,1)S(1)}, u32[]{:S(2)}, u32[]{:S(2)}) %collective-permute-start.51) | collective-permute-done | bytes 1048608 | tf_op jit(solution)/shard_map/ppermute | solution.py:40
  443.1 20.0 %collective-permute-done.54 = bf16[1024,512]{1,0:T(8,128)(2,1)S(1)} collective-permute-done((bf16[1024,512]{1,0:T(8,128)(2,1)S(1)}, bf16[1024,512]{1,0:T(8,128)(2,1)S(1)}, u32[]{:S(2)}, u32[]{:S(2)}) %collective-permute-start.54) | collective-permute-done | bytes 1048608 | tf_op jit(solution)/shard_map/ppermute | solution.py:40
  464.5 4.9 collective-permute-done.34
  476.2 10.5 %outer_attend_back.1 = (bf16[512,256]{1,0:T(8,128)(2,1)}, bf16[512,256]{1,0:T(8,128)(2,1)}, bf16[512,256]{1,0:T(8,128)(2,1)}) custom-call(s32[4]{0:T(128)} %copy-done.87, s32[1,512]{1,0:T(1,128)} %bitcast.247, bf16[512,768]{1,0:T(8,128)(2,1)} %convolution_convert_fusion.8.query_ref.key_ref.value_ref, ...), custom_call_target="tpu_custom_call" | custom-call | tf_op jit(solution)/shard_map/outer_attend_back/pallas_call | solution.py:236
  512.9 4.2 add_convert_fusion.1
  517.1 5.1 add_convert_fusion
  526.3 27.4 %collective-permute-done.39 = bf16[128,1024]{1,0:T(8,128)(2,1)S(1)} collective-permute-done((bf16[128,1024]{1,0:T(8,128)(2,1)S(1)}, bf16[128,1024]{1,0:T(8,128)(2,1)S(1)}, u32[]{:S(2)}, u32[]{:S(2)}) %collective-permute-start.39) | collective-permute-done | bytes 262176 | tf_op jit(solution)/shard_map/ppermute | solution.py:40
  561.7 4.6 collective-permute-done.41
  578.7 10.0 %collective-permute-done.56 = bf16[1024,128]{1,0:T(8,128)(2,1)S(1)} collective-permute-done((bf16[1024,128]{1,0:T(8,128)(2,1)}, bf16[1024,128]{1,0:T(8,128)(2,1)S(1)}, u32[]{:S(2)}, u32[]{:S(2)}) %collective-permute-start.56) | collective-permute-done | bytes 262176 | tf_op jit(solution)/shard_map/ppermute | solution.py:40
  593.6 43.5 %collective-permute-done.44 = f32[112,128]{1,0:T(8,128)S(1)} collective-permute-done((f32[112,128]{1,0:T(8,128)S(1)}, f32[112,128]{1,0:T(8,128)S(1)}, u32[]{:S(2)}, u32[]{:S(2)}) %collective-permute-start.44) | collective-permute-done | bytes 57376 | tf_op jit(solution)/shard_map/ppermute | solution.py:40
  641.0 8.3 %collective-permute-done.46 = bf16[768,256]{1,0:T(8,128)(2,1)S(1)} collective-permute-done((bf16[768,256]{1,0:T(8,128)(2,1)S(1)}, bf16[768,256]{1,0:T(8,128)(2,1)S(1)}, u32[]{:S(2)}, u32[]{:S(2)}) %collective-permute-start.46) | collective-permute-done | bytes 393248 | tf_op jit(solution)/shard_map/ppermute | solution.py:40
  652.2 15.9 %collective-permute-done.60 = bf16[768,512]{1,0:T(8,128)(2,1)S(1)} collective-permute-done((bf16[768,512]{1,0:T(8,128)(2,1)S(1)}, bf16[768,512]{1,0:T(8,128)(2,1)S(1)}, u32[]{:S(2)}, u32[]{:S(2)}) %collective-permute-start.60) | collective-permute-done | bytes 786464 | tf_op jit(solution)/shard_map/ppermute | solution.py:40
  677.2 8.2 %collective-permute-done.77 = bf16[1024,1024]{1,0:T(8,128)(2,1)S(1)} collective-permute-done((bf16[1024,1024]{1,0:T(8,128)(2,1)}, bf16[1024,1024]{1,0:T(8,128)(2,1)S(1)}, u32[]{:S(2)}, u32[]{:S(2)}) %collective-permute-start.77) | collective-permute-done | bytes 2097184 | tf_op jit(solution)/shard_map/ppermute | solution.py:40
  694.5 7.4 collective-permute-done.72
  704.9 16.4 %collective-permute-done.78 = bf16[1024,512]{1,0:T(8,128)(2,1)} collective-permute-done((bf16[1024,512]{1,0:T(8,128)(2,1)}, bf16[1024,512]{1,0:T(8,128)(2,1)}, u32[]{:S(2)}, u32[]{:S(2)}) %collective-permute-start.78) | collective-permute-done | bytes 1048608 | tf_op jit(solution)/shard_map/ppermute | solution.py:40
  725.9 13.6 %collective-permute-done.79 = bf16[1024,256]{1,0:T(8,128)(2,1)S(1)} collective-permute-done((bf16[1024,256]{1,0:T(8,128)(2,1)S(1)}, bf16[1024,256]{1,0:T(8,128)(2,1)S(1)}, u32[]{:S(2)}, u32[]{:S(2)}) %collective-permute-start.79) | collective-permute-done | bytes 524320 | tf_op jit(solution)/shard_map/ppermute | solution.py:40
  747.5 4.7 collective-permute-done.80
  (675 shorter events, 268.5 us)
Async XLA Ops:
  4.5 40.0 %collective-permute-start = (bf16[128,1024]{1,0:T(8,128)(2,1)}, bf16[128,1024]{1,0:T(8,128)(2,1)}, u32[]{:S(2)}, u32[]{:S(2)}) collective-permute-start(bf16[128,1024]{1,0:T(8,128)(2,1)} %fusion.64), channel_id=1, source_target_pairs={{0,2},{1,3},{2,0},{3,1},{4,6},{5,7},{6,4},{7,5},{8,10},{9,11},{10,... | collective-permute-start | bytes 786440 | tf_op jit(solution)/shard_map/ppermute | solution.py:40
  7.4 48.0 %collective-permute-start.1 = (bf16[128,1024]{1,0:T(8,128)(2,1)}, bf16[128,1024]{1,0:T(8,128)(2,1)}, u32[]{:S(2)}, u32[]{:S(2)}) collective-permute-start(bf16[128,1024]{1,0:T(8,128)(2,1)} %fusion.64), channel_id=1, source_target_pairs={{0,1},{1,0},{2,3},{3,2},{4,5},{5,4},{6,7},{7,6},{8,9},{9,8},{10,11... | collective-permute-start | bytes 786440 | tf_op jit(solution)/shard_map/ppermute | solution.py:40
  11.3 119.2 %collective-permute-start.12 = (bf16[1024,768]{1,0:T(8,128)(2,1)}, bf16[1024,768]{1,0:T(8,128)(2,1)}, u32[]{:S(2)}, u32[]{:S(2)}) collective-permute-start(bf16[1024,768]{1,0:T(8,128)(2,1)} %constant_dynamic-update-slice_fusion.3), channel_id=1, source_target_pairs={{0,1},{1,0},{2,3},{3,2},{4,5},{5,4},{6,7},{7,6},{8,9},{9,8},{10,11... | collective-permute-start | bytes 4718600 | tf_op jit(solution)/shard_map/ppermute | solution.py:40
  13.4 27.9 %collective-permute-start.13 = (bf16[128,768]{1,0:T(8,128)(2,1)}, bf16[128,768]{1,0:T(8,128)(2,1)}, u32[]{:S(2)}, u32[]{:S(2)}) collective-permute-start(bf16[128,768]{1,0:T(8,128)(2,1)} %constant_dynamic-slice_fusion.7), channel_id=1, source_target_pairs={{0,2},{1,3},{2,0},{3,1},{4,6},{5,7},{6,4},{7,5},{8,10},{9,11},{10,... | collective-permute-start | bytes 589832 | tf_op jit(solution)/shard_map/ppermute | solution.py:40
  13.4 220.9 %collective-permute-start.18 = (bf16[256,1024]{1,0:T(8,128)(2,1)}, bf16[256,1024]{1,0:T(8,128)(2,1)}, u32[]{:S(2)}, u32[]{:S(2)}) collective-permute-start(bf16[256,1024]{1,0:T(8,128)(2,1)} %param.42), channel_id=1, source_target_pairs={{0,1},{1,0},{2,3},{3,2},{4,5},{5,4},{6,7},{7,6},{8,9},{9,8},{10,11... | collective-permute-start | bytes 1572872 | tf_op jit(solution)/shard_map/ppermute | solution.py:40
  44.5 28.2 %collective-permute-start.19 = (bf16[288,1024]{1,0:T(8,128)(2,1)}, bf16[288,1024]{1,0:T(8,128)(2,1)}, u32[]{:S(2)}, u32[]{:S(2)}) collective-permute-start(bf16[288,1024]{1,0:T(8,128)(2,1)} %pad_maximum_fusion.10), channel_id=1, source_target_pairs={{0,2},{1,3},{2,0},{3,1},{4,6},{5,7},{6,4},{7,5},{8,10},{9,11},{10,... | collective-permute-start | bytes 1769480 | tf_op jit(solution)/shard_map/ppermute | solution.py:40
  72.7 208.8 %collective-permute-start.25 = (bf16[1024,1024]{1,0:T(8,128)(2,1)}, bf16[1024,1024]{1,0:T(8,128)(2,1)}, u32[]{:S(2)}, u32[]{:S(2)}) collective-permute-start(bf16[1024,1024]{1,0:T(8,128)(2,1)} %param.46), channel_id=1, source_target_pairs={{0,1},{1,0},{2,3},{3,2},{4,5},{5,4},{6,7},{7,6},{8,9},{9,8},{10,11... | collective-permute-start | bytes 6291464 | tf_op jit(solution)/shard_map/ppermute | solution.py:40
  79.7 28.7 %collective-permute-start.20 = (bf16[1,288,1024]{2,1,0:T(8,128)(2,1)}, bf16[1,288,1024]{2,1,0:T(8,128)(2,1)S(1)}, u32[]{:S(2)}, u32[]{:S(2)}) collective-permute-start(bf16[1,288,1024]{2,1,0:T(8,128)(2,1)} %bitcast.23), channel_id=1, source_target_pairs={{0,16},{4,20},{8,24},{12,28},{16,0},{20,4},{24,8},{28,12},{1,17},{... | collective-permute-start | bytes 1769480 | tf_op jit(solution)/shard_map/ppermute | solution.py:40
  87.4 21.0 %collective-permute-start.6 = (bf16[128,1024]{1,0:T(8,128)(2,1)S(1)}, bf16[128,1024]{1,0:T(8,128)(2,1)S(1)}, u32[]{:S(2)}, u32[]{:S(2)}) collective-permute-start(bf16[128,1024]{1,0:T(8,128)(2,1)S(1)} %multiply_convert_fusion.7), channel_id=1, source_target_pairs={{0,2},{1,3},{2,0},{3,1},{4,6},{5,7},{6,4},{7,5},{8,10},{9,11},{10,... | collective-permute-start | bytes 786440 | tf_op jit(solution)/shard_map/ppermute | solution.py:40
  110.2 156.1 %collective-permute-start.24 = (bf16[1024,1024]{1,0:T(8,128)(2,1)}, bf16[1024,1024]{1,0:T(8,128)(2,1)}, u32[]{:S(2)}, u32[]{:S(2)}) collective-permute-start(bf16[1024,1024]{1,0:T(8,128)(2,1)} %param.44), channel_id=1, source_target_pairs={{0,1},{1,0},{2,3},{3,2},{4,5},{5,4},{6,7},{7,6},{8,9},{9,8},{10,11... | collective-permute-start | bytes 6291464 | tf_op jit(solution)/shard_map/ppermute | solution.py:40
  110.3 19.9 %collective-permute-start.16 = (bf16[4,128,768]{2,1,0:T(8,128)(2,1)S(1)}, bf16[4,128,768]{2,1,0:T(8,128)(2,1)S(1)}, u32[]{:S(2)}, u32[]{:S(2)}) collective-permute-start(bf16[4,128,768]{2,1,0:T(8,128)(2,1)S(1)} %bitcast.236), channel_id=1, source_target_pairs={{0,4},{4,0},{8,12},{12,8},{16,20},{20,16},{24,28},{28,24},{1,5},{5... | collective-permute-start | bytes 2359304 | tf_op jit(solution)/shard_map/ppermute | solution.py:40
  134.2 28.0 %collective-permute-start.21 = (bf16[2,288,1024]{2,1,0:T(8,128)(2,1)S(1)}, bf16[2,288,1024]{2,1,0:T(8,128)(2,1)S(1)}, u32[]{:S(2)}, u32[]{:S(2)}) collective-permute-start(bf16[2,288,1024]{2,1,0:T(8,128)(2,1)S(1)} %maximum_bitcast_fusion), channel_id=1, source_target_pairs={{0,8},{4,12},{8,0},{12,4},{16,24},{20,28},{24,16},{28,20},{1,9},{5... | collective-permute-start | bytes 3538952 | tf_op jit(solution)/shard_map/ppermute | solution.py:40
  140.8 23.5 %collective-permute-start.17 = (bf16[1024,768]{1,0:T(8,128)(2,1)S(1)}, bf16[1024,768]{1,0:T(8,128)(2,1)S(1)}, u32[]{:S(2)}, u32[]{:S(2)}) collective-permute-start(bf16[1024,768]{1,0:T(8,128)(2,1)S(1)} %bitcast.228), channel_id=1, source_target_pairs={{0,1},{1,0},{2,3},{3,2},{4,5},{5,4},{6,7},{7,6},{8,9},{9,8},{10,11... | collective-permute-start | bytes 4718600 | tf_op jit(solution)/shard_map/ppermute | solution.py:40
  162.6 52.4 %collective-permute-start.22 = (bf16[4,288,1024]{2,1,0:T(8,128)(2,1)S(1)}, bf16[4,288,1024]{2,1,0:T(8,128)(2,1)S(1)}, u32[]{:S(2)}, u32[]{:S(2)}) collective-permute-start(bf16[4,288,1024]{2,1,0:T(8,128)(2,1)S(1)} %bitcast.226), channel_id=1, source_target_pairs={{0,4},{4,0},{8,12},{12,8},{16,20},{20,16},{24,28},{28,24},{1,5},{5... | collective-permute-start | bytes 7077896 | tf_op jit(solution)/shard_map/ppermute | solution.py:40
  217.3 17.1 %collective-permute-start.23 = (bf16[256,1024]{1,0:T(8,128)(2,1)}, bf16[256,1024]{1,0:T(8,128)(2,1)}, u32[]{:S(2)}, u32[]{:S(2)}) collective-permute-start(bf16[256,1024]{1,0:T(8,128)(2,1)} %bitcast.34), channel_id=1, source_target_pairs={{0,1},{1,0},{2,3},{3,2},{4,5},{5,4},{6,7},{7,6},{8,9},{9,8},{10,11... | collective-permute-start | bytes 1572872 | tf_op jit(solution)/shard_map/ppermute | solution.py:40
  233.9 75.7 %collective-permute-start.27 = (bf16[1024,1024]{1,0:T(8,128)(2,1)}, bf16[1024,1024]{1,0:T(8,128)(2,1)}, u32[]{:S(2)}, u32[]{:S(2)}) collective-permute-start(bf16[1024,1024]{1,0:T(8,128)(2,1)} %bitcast.39), channel_id=1, source_target_pairs={{0,1},{1,0},{2,3},{3,2},{4,5},{5,4},{6,7},{7,6},{8,9},{9,8},{10,11... | collective-permute-start | bytes 6291464 | tf_op jit(solution)/shard_map/ppermute | solution.py:40
  234.4 72.3 %collective-permute-start.26 = (bf16[1024,1024]{1,0:T(8,128)(2,1)}, bf16[1024,1024]{1,0:T(8,128)(2,1)}, u32[]{:S(2)}, u32[]{:S(2)}) collective-permute-start(bf16[1024,1024]{1,0:T(8,128)(2,1)} %bitcast.37), channel_id=1, source_target_pairs={{0,1},{1,0},{2,3},{3,2},{4,5},{5,4},{6,7},{7,6},{8,9},{9,8},{10,11... | collective-permute-start | bytes 6291464 | tf_op jit(solution)/shard_map/ppermute | solution.py:40
  353.0 30.9 %collective-permute-start.28 = (bf16[128,1024]{1,0:T(8,128)(2,1)}, bf16[128,1024]{1,0:T(8,128)(2,1)}, u32[]{:S(2)}, u32[]{:S(2)}) collective-permute-start(bf16[128,1024]{1,0:T(8,128)(2,1)} %fusion.102), channel_id=1, source_target_pairs={{0,2},{1,3},{2,0},{3,1},{4,6},{5,7},{6,4},{7,5},{8,10},{9,11},{10,... | collective-permute-start | bytes 786440 | tf_op jit(solution)/shard_map/ppermute | solution.py:40
  353.5 31.0 %collective-permute-start.29 = (bf16[128,1024]{1,0:T(8,128)(2,1)}, bf16[128,1024]{1,0:T(8,128)(2,1)}, u32[]{:S(2)}, u32[]{:S(2)}) collective-permute-start(bf16[128,1024]{1,0:T(8,128)(2,1)} %fusion.102), channel_id=1, source_target_pairs={{0,1},{1,0},{2,3},{3,2},{4,5},{5,4},{6,7},{7,6},{8,9},{9,8},{10,11... | collective-permute-start | bytes 786440 | tf_op jit(solution)/shard_map/ppermute | solution.py:40
  373.1 96.3 %collective-permute-start.58 = (bf16[768,1024]{1,0:T(8,128)(2,1)}, bf16[768,1024]{1,0:T(8,128)(2,1)}, u32[]{:S(2)}, u32[]{:S(2)}) collective-permute-start(bf16[768,1024]{1,0:T(8,128)(2,1)} %convolution_convert_fusion.5), channel_id=1, source_target_pairs={{0,1},{1,0},{2,3},{3,2},{4,5},{5,4},{6,7},{7,6},{8,9},{9,8},{10,11... | collective-permute-start | bytes 4718600 | tf_op jit(solution)/shard_map/ppermute | solution.py:40
  375.8 261.2 %collective-permute-start.57 = (bf16[768,1024]{1,0:T(8,128)(2,1)}, bf16[768,1024]{1,0:T(8,128)(2,1)}, u32[]{:S(2)}, u32[]{:S(2)}) collective-permute-start(bf16[768,1024]{1,0:T(8,128)(2,1)} %convolution_convert_fusion.6), channel_id=1, source_target_pairs={{0,1},{1,0},{2,3},{3,2},{4,5},{5,4},{6,7},{7,6},{8,9},{9,8},{10,11... | collective-permute-start | bytes 4718600 | tf_op jit(solution)/shard_map/ppermute | solution.py:40
  378.6 15.5 %collective-permute-start.64 = (bf16[256,1024]{1,0:T(8,128)(2,1)}, bf16[256,1024]{1,0:T(8,128)(2,1)}, u32[]{:S(2)}, u32[]{:S(2)}) collective-permute-start(bf16[256,1024]{1,0:T(8,128)(2,1)} %convolution_convert_fusion.9), channel_id=1, source_target_pairs={{0,1},{1,0},{2,3},{3,2},{4,5},{5,4},{6,7},{7,6},{8,9},{9,8},{10,11... | collective-permute-start | bytes 1572872 | tf_op jit(solution)/shard_map/ppermute | solution.py:40
  398.7 16.9 %collective-permute-start.33 = (bf16[128,1024]{1,0:T(8,128)(2,1)S(1)}, bf16[128,1024]{1,0:T(8,128)(2,1)S(1)}, u32[]{:S(2)}, u32[]{:S(2)}) collective-permute-start(bf16[128,1024]{1,0:T(8,128)(2,1)S(1)} %fusion.72), channel_id=1, source_target_pairs={{0,2},{1,3},{2,0},{3,1},{4,6},{5,7},{6,4},{7,5},{8,10},{9,11},{10,... | collective-permute-start | bytes 786440 | tf_op jit(solution)/shard_map/ppermute | solution.py:40
  412.6 30.0 %collective-permute-start.51 = (bf16[1024,512]{1,0:T(8,128)(2,1)S(1)}, bf16[1024,512]{1,0:T(8,128)(2,1)S(1)}, u32[]{:S(2)}, u32[]{:S(2)}) collective-permute-start(bf16[1024,512]{1,0:T(8,128)(2,1)S(1)} %dynamic-slice_convert_fusion.3), channel_id=1, source_target_pairs={{0,4},{4,0},{8,12},{12,8},{16,20},{20,16},{24,28},{28,24},{1,5},{5... | collective-permute-start | bytes 3145736 | tf_op jit(solution)/shard_map/ppermute | solution.py:40
  415.6 47.5 %collective-permute-start.54 = (bf16[1024,512]{1,0:T(8,128)(2,1)S(1)}, bf16[1024,512]{1,0:T(8,128)(2,1)S(1)}, u32[]{:S(2)}, u32[]{:S(2)}) collective-permute-start(bf16[1024,512]{1,0:T(8,128)(2,1)S(1)} %dynamic-slice_convert_fusion.2), channel_id=1, source_target_pairs={{0,4},{4,0},{8,12},{12,8},{16,20},{20,16},{24,28},{28,24},{1,5},{5... | collective-permute-start | bytes 3145736 | tf_op jit(solution)/shard_map/ppermute | solution.py:40
  431.4 80.6 %collective-permute-start.70 = (bf16[1024,1024]{1,0:T(8,128)(2,1)}, bf16[1024,1024]{1,0:T(8,128)(2,1)}, u32[]{:S(2)}, u32[]{:S(2)}) collective-permute-start(bf16[1024,1024]{1,0:T(8,128)(2,1)} %convolution_convert_fusion.3), channel_id=1, source_target_pairs={{0,1},{1,0},{2,3},{3,2},{4,5},{5,4},{6,7},{7,6},{8,9},{9,8},{10,11... | collective-permute-start | bytes 6291464 | tf_op jit(solution)/shard_map/ppermute | solution.py:40
  442.6 74.5 %collective-permute-start.76 = (bf16[1024,1024]{1,0:T(8,128)(2,1)}, bf16[1024,1024]{1,0:T(8,128)(2,1)}, u32[]{:S(2)}, u32[]{:S(2)}) collective-permute-start(bf16[1024,1024]{1,0:T(8,128)(2,1)} %convolution_convert_fusion.1), channel_id=1, source_target_pairs={{0,1},{1,0},{2,3},{3,2},{4,5},{5,4},{6,7},{7,6},{8,9},{9,8},{10,11... | collective-permute-start | bytes 6291464 | tf_op jit(solution)/shard_map/ppermute | solution.py:40
  473.6 48.6 %collective-permute-start.52 = (bf16[1024,256]{1,0:T(8,128)(2,1)S(1)}, bf16[1024,256]{1,0:T(8,128)(2,1)}, u32[]{:S(2)}, u32[]{:S(2)}) collective-permute-start(bf16[1024,256]{1,0:T(8,128)(2,1)S(1)} %dynamic-slice_convert_fusion.9), channel_id=1, source_target_pairs={{0,8},{4,12},{8,0},{12,4},{16,24},{20,28},{24,16},{28,20},{1,9},{5... | collective-permute-start | bytes 1572872 | tf_op jit(solution)/shard_map/ppermute | solution.py:40
  511.4 49.8 %collective-permute-start.55 = (bf16[1024,256]{1,0:T(8,128)(2,1)S(1)}, bf16[1024,256]{1,0:T(8,128)(2,1)S(1)}, u32[]{:S(2)}, u32[]{:S(2)}) collective-permute-start(bf16[1024,256]{1,0:T(8,128)(2,1)S(1)} %dynamic-slice_convert_fusion.8), channel_id=1, source_target_pairs={{0,8},{4,12},{8,0},{12,4},{16,24},{20,28},{24,16},{28,20},{1,9},{5... | collective-permute-start | bytes 1572872 | tf_op jit(solution)/shard_map/ppermute | solution.py:40
  512.1 126.0 %collective-permute-start.59 = (bf16[768,1024]{1,0:T(8,128)(2,1)}, bf16[768,1024]{1,0:T(8,128)(2,1)}, u32[]{:S(2)}, u32[]{:S(2)}) collective-permute-start(bf16[768,1024]{1,0:T(8,128)(2,1)} %add_convert_fusion.2), channel_id=1, source_target_pairs={{0,2},{1,3},{2,0},{3,1},{4,6},{5,7},{6,4},{7,5},{8,10},{9,11},{10,... | collective-permute-start | bytes 4718600 | tf_op jit(solution)/shard_map/ppermute | solution.py:40
  522.3 31.4 %collective-permute-start.39 = (bf16[128,1024]{1,0:T(8,128)(2,1)S(1)}, bf16[128,1024]{1,0:T(8,128)(2,1)S(1)}, u32[]{:S(2)}, u32[]{:S(2)}) collective-permute-start(bf16[128,1024]{1,0:T(8,128)(2,1)S(1)} %fusion.70), channel_id=1, source_target_pairs={{0,2},{1,3},{2,0},{3,1},{4,6},{5,7},{6,4},{7,5},{8,10},{9,11},{10,... | collective-permute-start | bytes 786440 | tf_op jit(solution)/shard_map/ppermute | solution.py:40
  524.7 65.8 %collective-permute-start.45 = (bf16[768,512]{1,0:T(8,128)(2,1)}, bf16[768,512]{1,0:T(8,128)(2,1)}, u32[]{:S(2)}, u32[]{:S(2)}) collective-permute-start(bf16[768,512]{1,0:T(8,128)(2,1)} %dynamic-slice_convert_fusion.5), channel_id=1, source_target_pairs={{0,4},{4,0},{8,12},{12,8},{16,20},{20,16},{24,28},{28,24},{1,5},{5... | collective-permute-start | bytes 2359304 | tf_op jit(solution)/shard_map/ppermute | solution.py:40
  558.3 17.4 %collective-permute-start.53 = (bf16[1024,128]{1,0:T(8,128)(2,1)S(1)}, bf16[1024,128]{1,0:T(8,128)(2,1)S(1)}, u32[]{:S(2)}, u32[]{:S(2)}) collective-permute-start(bf16[1024,128]{1,0:T(8,128)(2,1)S(1)} %dynamic-slice_convert_fusion.16), channel_id=1, source_target_pairs={{0,16},{4,20},{8,24},{12,28},{16,0},{20,4},{24,8},{28,12},{1,17},{... | collective-permute-start | bytes 786440 | tf_op jit(solution)/shard_map/ppermute | solution.py:40
  573.6 15.1 %collective-permute-start.56 = (bf16[1024,128]{1,0:T(8,128)(2,1)}, bf16[1024,128]{1,0:T(8,128)(2,1)S(1)}, u32[]{:S(2)}, u32[]{:S(2)}) collective-permute-start(bf16[1024,128]{1,0:T(8,128)(2,1)} %dynamic-slice_convert_fusion.15), channel_id=1, source_target_pairs={{0,16},{4,20},{8,24},{12,28},{16,0},{20,4},{24,8},{28,12},{1,17},{... | collective-permute-start | bytes 786440 | tf_op jit(solution)/shard_map/ppermute | solution.py:40
  575.8 95.2 %collective-permute-start.69 = (bf16[1024,1024]{1,0:T(8,128)(2,1)}, bf16[1024,1024]{1,0:T(8,128)(2,1)}, u32[]{:S(2)}, u32[]{:S(2)}) collective-permute-start(bf16[1024,1024]{1,0:T(8,128)(2,1)} %convolution_convert_fusion.4), channel_id=1, source_target_pairs={{0,1},{1,0},{2,3},{3,2},{4,5},{5,4},{6,7},{7,6},{8,9},{9,8},{10,11... | collective-permute-start | bytes 6291464 | tf_op jit(solution)/shard_map/ppermute | solution.py:40
  588.7 83.7 %collective-permute-start.71 = (bf16[1024,1024]{1,0:T(8,128)(2,1)}, bf16[1024,1024]{1,0:T(8,128)(2,1)S(1)}, u32[]{:S(2)}, u32[]{:S(2)}) collective-permute-start(bf16[1024,1024]{1,0:T(8,128)(2,1)} %add_convert_fusion.1), channel_id=1, source_target_pairs={{0,2},{1,3},{2,0},{3,1},{4,6},{5,7},{6,4},{7,5},{8,10},{9,11},{10,... | collective-permute-start | bytes 6291464 | tf_op jit(solution)/shard_map/ppermute | solution.py:40
  590.5 46.5 %collective-permute-start.44 = (f32[112,128]{1,0:T(8,128)S(1)}, f32[112,128]{1,0:T(8,128)S(1)}, u32[]{:S(2)}, u32[]{:S(2)}) collective-permute-start(f32[112,128]{1,0:T(8,128)S(1)} %add.575), channel_id=1, source_target_pairs={{0,2},{1,3},{2,0},{3,1},{4,6},{5,7},{6,4},{7,5},{8,10},{9,11},{10,... | collective-permute-start | bytes 172040 | tf_op jit(solution)/shard_map/ppermute | solution.py:40
  637.1 40.1 %collective-permute-start.75 = (bf16[1024,1024]{1,0:T(8,128)(2,1)S(1)}, bf16[1024,1024]{1,0:T(8,128)(2,1)S(1)}, u32[]{:S(2)}, u32[]{:S(2)}) collective-permute-start(bf16[1024,1024]{1,0:T(8,128)(2,1)S(1)} %copy-done.111), channel_id=1, source_target_pairs={{0,1},{1,0},{2,3},{3,2},{4,5},{5,4},{6,7},{7,6},{8,9},{9,8},{10,11... | collective-permute-start | bytes 6291464 | tf_op jit(solution)/shard_map/ppermute | solution.py:40
  637.1 48.3 %collective-permute-start.77 = (bf16[1024,1024]{1,0:T(8,128)(2,1)}, bf16[1024,1024]{1,0:T(8,128)(2,1)S(1)}, u32[]{:S(2)}, u32[]{:S(2)}) collective-permute-start(bf16[1024,1024]{1,0:T(8,128)(2,1)} %add_convert_fusion), channel_id=1, source_target_pairs={{0,2},{1,3},{2,0},{3,1},{4,6},{5,7},{6,4},{7,5},{8,10},{9,11},{10,... | collective-permute-start | bytes 6291464 | tf_op jit(solution)/shard_map/ppermute | solution.py:40
  649.3 18.8 %collective-permute-start.60 = (bf16[768,512]{1,0:T(8,128)(2,1)S(1)}, bf16[768,512]{1,0:T(8,128)(2,1)S(1)}, u32[]{:S(2)}, u32[]{:S(2)}) collective-permute-start(bf16[768,512]{1,0:T(8,128)(2,1)S(1)} %dynamic-slice_convert_fusion.4), channel_id=1, source_target_pairs={{0,4},{4,0},{8,12},{12,8},{16,20},{20,16},{24,28},{28,24},{1,5},{5... | collective-permute-start | bytes 2359304 | tf_op jit(solution)/shard_map/ppermute | solution.py:40
  668.2 22.5 %collective-permute-start.47 = (bf16[768,128]{1,0:T(8,128)(2,1)S(1)}, bf16[768,128]{1,0:T(8,128)(2,1)S(1)}, u32[]{:S(2)}, u32[]{:S(2)}) collective-permute-start(bf16[768,128]{1,0:T(8,128)(2,1)S(1)} %dynamic-slice_convert_fusion.19), channel_id=1, source_target_pairs={{0,16},{4,20},{8,24},{12,28},{16,0},{20,4},{24,8},{28,12},{1,17},{... | collective-permute-start | bytes 589832 | tf_op jit(solution)/shard_map/ppermute | solution.py:40
  671.0 22.1 %collective-permute-start.61 = (bf16[768,256]{1,0:T(8,128)(2,1)}, bf16[768,256]{1,0:T(8,128)(2,1)}, u32[]{:S(2)}, u32[]{:S(2)}) collective-permute-start(bf16[768,256]{1,0:T(8,128)(2,1)} %dynamic-slice_convert_fusion.10), channel_id=1, source_target_pairs={{0,8},{4,12},{8,0},{12,4},{16,24},{20,28},{24,16},{28,20},{1,9},{5... | collective-permute-start | bytes 1179656 | tf_op jit(solution)/shard_map/ppermute | solution.py:40
  675.6 26.3 %collective-permute-start.72 = (bf16[1024,512]{1,0:T(8,128)(2,1)S(1)}, bf16[1024,512]{1,0:T(8,128)(2,1)}, u32[]{:S(2)}, u32[]{:S(2)}) collective-permute-start(bf16[1024,512]{1,0:T(8,128)(2,1)S(1)} %dynamic-slice_convert_fusion.1), channel_id=1, source_target_pairs={{0,4},{4,0},{8,12},{12,8},{16,20},{20,16},{24,28},{28,24},{1,5},{5... | collective-permute-start | bytes 3145736 | tf_op jit(solution)/shard_map/ppermute | solution.py:40
  689.2 32.1 %collective-permute-start.78 = (bf16[1024,512]{1,0:T(8,128)(2,1)}, bf16[1024,512]{1,0:T(8,128)(2,1)}, u32[]{:S(2)}, u32[]{:S(2)}) collective-permute-start(bf16[1024,512]{1,0:T(8,128)(2,1)} %dynamic-slice_convert_fusion), channel_id=1, source_target_pairs={{0,4},{4,0},{8,12},{12,8},{16,20},{20,16},{24,28},{28,24},{1,5},{5... | collective-permute-start | bytes 3145736 | tf_op jit(solution)/shard_map/ppermute | solution.py:40
  694.4 29.5 %collective-permute-start.62 = (bf16[768,128]{1,0:T(8,128)(2,1)S(1)}, bf16[768,128]{1,0:T(8,128)(2,1)S(1)}, u32[]{:S(2)}, u32[]{:S(2)}) collective-permute-start(bf16[768,128]{1,0:T(8,128)(2,1)S(1)} %dynamic-slice_convert_fusion.18), channel_id=1, source_target_pairs={{0,16},{4,20},{8,24},{12,28},{16,0},{20,4},{24,8},{28,12},{1,17},{... | collective-permute-start | bytes 589832 | tf_op jit(solution)/shard_map/ppermute | solution.py:40
  704.2 19.8 %collective-permute-start.73 = (bf16[1024,256]{1,0:T(8,128)(2,1)S(1)}, bf16[1024,256]{1,0:T(8,128)(2,1)S(1)}, u32[]{:S(2)}, u32[]{:S(2)}) collective-permute-start(bf16[1024,256]{1,0:T(8,128)(2,1)S(1)} %dynamic-slice_convert_fusion.7), channel_id=1, source_target_pairs={{0,8},{4,12},{8,0},{12,4},{16,24},{20,28},{24,16},{28,20},{1,9},{5... | collective-permute-start | bytes 1572872 | tf_op jit(solution)/shard_map/ppermute | solution.py:40
  722.9 16.5 %collective-permute-start.79 = (bf16[1024,256]{1,0:T(8,128)(2,1)S(1)}, bf16[1024,256]{1,0:T(8,128)(2,1)S(1)}, u32[]{:S(2)}, u32[]{:S(2)}) collective-permute-start(bf16[1024,256]{1,0:T(8,128)(2,1)S(1)} %dynamic-slice_convert_fusion.6), channel_id=1, source_target_pairs={{0,8},{4,12},{8,0},{12,4},{16,24},{20,28},{24,16},{28,20},{1,9},{5... | collective-permute-start | bytes 1572872 | tf_op jit(solution)/shard_map/ppermute | solution.py:40
  724.9 18.7 %collective-permute-start.74 = (bf16[1024,128]{1,0:T(8,128)(2,1)}, bf16[1024,128]{1,0:T(8,128)(2,1)}, u32[]{:S(2)}, u32[]{:S(2)}) collective-permute-start(bf16[1024,128]{1,0:T(8,128)(2,1)} %dynamic-slice_convert_fusion.13), channel_id=1, source_target_pairs={{0,16},{4,20},{8,24},{12,28},{16,0},{20,4},{24,8},{28,12},{1,17},{... | collective-permute-start | bytes 786440 | tf_op jit(solution)/shard_map/ppermute | solution.py:40
  (165 other events, 1502.4 us)
